TPU v7x, 128 devices: a whole 4x4x4 slice. The times are simulated.
128 devices in a mesh: seq: 16 (over x, y), head: 8 (over z, core).
Axes of the slice: x: 4, y: 4, z: 4, core: 2. Of those that a mesh axis runs over, the one named last changes fastest.
Arguments:
- hidden_in: bfloat16 [16384, 2048], P('seq', 'head'), may hold values from -9 to 9
- w_query: bfloat16 [2048, 2048], P(None, 'head'), may hold values from -0.125 to 0.125
- w_key: bfloat16 [2048, 2048], P(None, 'head'), may hold values from -0.125 to 0.125
- w_value: bfloat16 [2048, 4096], P(None, 'head'), may hold values from -0.125 to 0.125
- w_gate: bfloat16 [2048, 4096], P(None, 'head'), may hold values from -0.125 to 0.125
- w_beta: bfloat16 [2048, 32], P(None, 'head'), may hold values from -0.8 to 0.8
- w_alpha: bfloat16 [2048, 32], P(None, 'head'), may hold values from -0.125 to 0.125
- dt_bias: float32 [32], P('head'), may hold values from -1 to 1
- head_decay: float32 [32], P('head'), may hold values from 6.1035156e-06 to 0.05
- conv_query: bfloat16 [4, 2048], P(None, 'head'), may hold values from -3 to 3
- conv_key: bfloat16 [4, 2048], P(None, 'head'), may hold values from -3 to 3
- conv_value: bfloat16 [4, 4096], P(None, 'head'), may hold values from -3 to 3
- norm_weight: float32 [128], replicated, may hold values from 0.25 to 1.75
- w_out: bfloat16 [4096, 2048], P('head'), may hold values from -0.09375 to 0.09375
- prompt_lengths: int32 [6], replicated, may hold values from 1 to 8192, 16384 in all
Outputs:
- layer_out: bfloat16 [16384, 2048], P('seq', 'head')
Inputs may be any that keep to these rules, and one draw needn't show every extreme that they name: `prompt_lengths`: the lengths sum to 16384; the longest is 8192.
All inputs are finite; a program needn't handle non-finite values.
Results may differ from a plain program's by a relative error of at most 0.018.
Values may be sent and summed in bfloat16 or wider, within the bound.
A program may use at most 128 MiB of HBM per device.

v0:
```python
import jax
import jax.numpy as jnp
from jax import lax
from jax.sharding import PartitionSpec as P

KHEADS = 16
VHEADS = 32
HEAD_DIM = 128
CONV = 4
BLOCK = 64


highest = lax.Precision.HIGHEST


def passed_along(array, axis, by):
    size = lax.axis_size(axis)
    pairs = [(i, i + by) for i in range(size) if 0 <= i + by < size]
    return lax.ppermute(array, axis, pairs)


def composed_product(form, left_side, right_side):
    return jnp.einsum(form, left_side, right_side, precision=highest)


def unit_scale(values_in):
    return values_in * lax.rsqrt(jnp.sum(values_in * values_in, axis=-1, keepdims=True) + 1e-06)


def block_terms(queries, keys_in, values_in, betas, log_decay, resets):
    width_in = queries.shape[1]
    segment = jnp.cumsum(resets)
    cumulative = jnp.cumsum(log_decay, axis=1)
    spread = cumulative[:, :, None] - cumulative[:, None, :]
    position = jnp.arange(width_in)
    causal = position[:, None] >= position[None, :]
    strictly = position[:, None] > position[None, :]
    joined = segment[:, None] == segment[None, :]
    factor = jnp.where((causal & joined)[None], jnp.exp(jnp.minimum(spread, 0.0)), 0.0)
    scaled = jnp.where(segment[None, :] == 0, jnp.exp(cumulative), 0.0)
    similar = composed_product("hik,hjk->hij", keys_in, keys_in)
    system = jnp.eye(width_in, dtype=queries.dtype)[None] + betas[:, :, None] * jnp.where(
        strictly[None], factor * similar, 0.0
    )
    right_hand = jnp.concatenate(
        [betas[:, :, None] * values_in, (betas * scaled)[:, :, None] * keys_in], axis=-1
    )
    solved = jax.scipy.linalg.solve_triangular(system, right_hand, lower=True, unit_diagonal=True)
    value_width = values_in.shape[-1]
    corrected_values = solved[..., :value_width]
    w_keys = solved[..., value_width:]
    attend = factor * composed_product("hik,hjk->hij", queries, keys_in)
    trailing_keys = factor[:, -1, :, None] * keys_in
    identity_k = jnp.eye(keys_in.shape[-1], dtype=queries.dtype)
    state_transfer = scaled[:, -1, None, None] * identity_k[None] - composed_product(
        "hck,hcl->hkl", trailing_keys, w_keys
    )
    inserted_values = composed_product("iws,iwe->ise", trailing_keys, corrected_values)
    producer_fn = scaled[:, :, None] * queries - composed_product("hij,hjk->hik", attend, w_keys)
    self_output = composed_product("hij,hjv->hiv", attend, corrected_values)
    return (producer_fn, self_output, state_transfer, inserted_values)


def short_conv(raw_in, prefix_rows, taps, positions, starts):
    reach = taps.shape[0]
    row_count = raw_in.shape[0]
    extended = jnp.concatenate([prefix_rows, raw_in], axis=0).astype(jnp.float32)
    running = jnp.zeros(raw_in.shape, jnp.float32)
    for tap_index in range(reach):
        tap_lag = reach - 1 - tap_index
        inside = (positions - tap_lag >= starts).astype(jnp.float32)
        running = (
            running
            + taps[tap_index].astype(jnp.float32)[None, :]
            * extended[tap_index : tap_index + row_count]
            * inside[:, None]
        )
    return jax.nn.silu(running)


def to_blocks(array_in):
    row_count, head_count, width_in = array_in.shape
    return array_in.reshape(row_count // BLOCK, BLOCK, head_count, width_in).transpose(0, 2, 1, 3)


def to_blocks_flat(array_in):
    row_count, head_count = array_in.shape
    return array_in.reshape(row_count // BLOCK, BLOCK, head_count).transpose(0, 2, 1)


def per_device(
    hidden_in,
    w_query,
    w_key,
    w_value,
    w_gate,
    w_beta,
    w_alpha,
    dt_bias,
    head_decay,
    conv_query,
    conv_key,
    conv_value,
    norm_weight,
    w_out,
    prompt_lengths,
):
    row_count = hidden_in.shape[0]
    key_cols = w_query.shape[1]
    value_cols = w_value.shape[1]
    local_kheads = key_cols // HEAD_DIM
    local_heads = value_cols // HEAD_DIM
    weights = (w_query, w_key, w_value, w_gate, w_beta, w_alpha)
    columns_in = lax.all_gather(hidden_in, "head", axis=1, tiled=True)
    sums_q, sums_k, sums_v, sums_z, sums_b, sums_a = tuple(
        (jnp.dot(columns_in, weight, preferred_element_type=jnp.float32) for weight in weights)
    )
    raw_q = sums_q.astype(jnp.bfloat16)
    raw_k = sums_k.astype(jnp.bfloat16)
    raw_v = sums_v.astype(jnp.bfloat16)
    raw_z = sums_z.astype(jnp.bfloat16)
    betas = jax.nn.sigmoid(sums_b)
    log_decay = -head_decay[None, :] * jax.nn.softplus(sums_a + dt_bias[None, :])
    tails = jnp.concatenate(
        [
            raw_q[row_count - (CONV - 1) :],
            raw_k[row_count - (CONV - 1) :],
            raw_v[row_count - (CONV - 1) :],
        ],
        axis=1,
    )
    received = passed_along(tails, "seq", 1)
    positions = lax.axis_index("seq") * row_count + jnp.arange(row_count, dtype=jnp.int32)
    offsets = jnp.cumsum(prompt_lengths) - prompt_lengths
    starts = jnp.max(jnp.where(offsets[None, :] <= positions[:, None], offsets[None, :], 0), axis=1)
    resets = (positions == starts).astype(jnp.float32)
    conv_q = short_conv(raw_q, received[:, :key_cols], conv_query, positions, starts)
    conv_k = short_conv(raw_k, received[:, key_cols : 2 * key_cols], conv_key, positions, starts)
    conv_v = short_conv(raw_v, received[:, 2 * key_cols :], conv_value, positions, starts)
    group_ratio = VHEADS // KHEADS
    queries = jnp.repeat(
        unit_scale(conv_q.reshape(row_count, local_kheads, HEAD_DIM)), group_ratio, axis=1
    ) * HEAD_DIM ** (-0.5)
    keys_all = jnp.repeat(
        unit_scale(conv_k.reshape(row_count, local_kheads, HEAD_DIM)), group_ratio, axis=1
    )
    values_all = conv_v.reshape(row_count, local_heads, HEAD_DIM)
    blocks = (
        to_blocks(queries),
        to_blocks(keys_all),
        to_blocks(values_all),
        to_blocks_flat(betas),
        to_blocks_flat(log_decay),
        resets.reshape(row_count // BLOCK, BLOCK),
    )
    identity_k = jnp.eye(HEAD_DIM, dtype=jnp.float32)
    identity_heads = jnp.broadcast_to(identity_k[None], (local_heads, HEAD_DIM, HEAD_DIM))
    zero_state = jnp.zeros((local_heads, HEAD_DIM, HEAD_DIM), jnp.float32)

    def advance(carried, pieces):
        across_blocks, passed_state = carried
        producer_fn, self_output, state_transfer, inserted_values = block_terms(*pieces)
        block_result = composed_product("upj,ujt->upt", producer_fn, passed_state) + self_output
        lifted = composed_product("hik,hkl->hil", producer_fn, across_blocks)
        next_through = composed_product("hkl,hlm->hkm", state_transfer, across_blocks)
        following_state = (
            composed_product("ryp,rpj->ryj", state_transfer, passed_state) + inserted_values
        )
        return ((next_through, following_state), (block_result, lifted))

    (across_blocks, block_local_state), (block_results, raised_everything) = lax.scan(
        advance, (identity_heads, zero_state), blocks
    )

    def turn(turn_index, arriving):
        departing = composed_product("ryp,rpj->ryj", across_blocks, arriving) + block_local_state
        return passed_along(departing.astype(jnp.bfloat16), "seq", 1).astype(departing.dtype)

    arriving_state = lax.fori_loop(0, lax.axis_size("seq") - 1, turn, zero_state)
    attention_result = block_results + composed_product(
        "engs,nsa->enga", raised_everything, arriving_state
    )
    attention_result = attention_result.transpose(0, 2, 1, 3).reshape(
        row_count, local_heads, HEAD_DIM
    )
    variance = jnp.mean(attention_result * attention_result, axis=-1, keepdims=True)
    gate_vals = raw_z.astype(jnp.float32).reshape(row_count, local_heads, HEAD_DIM)
    normed = (
        attention_result
        * lax.rsqrt(variance + 1e-06)
        * norm_weight[None, None, :]
        * jax.nn.silu(gate_vals)
    ).astype(jnp.bfloat16)
    normed = normed.reshape(row_count, local_heads * HEAD_DIM)
    partial_sum = jnp.dot(normed, w_out, preferred_element_type=jnp.float32)
    return lax.psum_scatter(
        partial_sum.astype(jnp.bfloat16), "head", scatter_dimension=1, tiled=True
    )


def solution(mesh):
    in_specs = (
        P("seq", "head"),
        P(None, "head"),
        P(None, "head"),
        P(None, "head"),
        P(None, "head"),
        P(None, "head"),
        P(None, "head"),
        P("head"),
        P("head"),
        P(None, "head"),
        P(None, "head"),
        P(None, "head"),
        P(),
        P("head", None),
        P(),
    )
    out_specs = P("seq", "head")
    return jax.shard_map(
        per_device, mesh=mesh, in_specs=in_specs, out_specs=out_specs, check_vma=False
    )
```

profile of v0, /device:TPU:0, one launch (start us, length us, event | category | flops | bytes accessed | tf_op | source)
XLA Modules:
  0.0 838.5 jit_solution(10679672164445779595)
XLA Ops:
  14.6 32.7 %all-gather.2.cloned.1.call-done = bf16[1024,2048]{1,0:T(8,128)(2,1)} async-done(((bf16[1024,256]{1,0:T(8,128)(2,1)}), bf16[1024,2048]{1,0:T(8,128)(2,1)}) %all-gather.2.cloned.1.call-update) | async-done | bytes 4194320 | tf_op jit(solution)/shard_map/all_gather | solution.py:114
  47.3 5.3 convolution_convert_fusion.2
  56.3 3.6 collective-permute-start.1
  61.2 3.4 fusion.69
  69.3 2.7 reshape.278
  85.9 2.8 divide_multiply_fusion
  88.8 2.9 reshape_reshape.7
  91.7 3.4 copy.89
  98.0 530.5 %while.28 = (s32[]{:T(128)}, f32[4,128,128]{2,1,0:T(8,128)S(1)}, f32[4,128,128]{2,1,0:T(8,128)S(1)}, f32[16,4,64,128]{3,2,0,1:T(8,128)}, f32[16,4,64,128]{3,2,0,...) while((s32[]{:T(128)}, f32[4,128,128]{2,1,0:T(8,128)S(1)}, ...), condition=%wide.region_7.8_spmd.clone, body=%wide.region_4.7_spmd.clone.sunk | while | flops 554623296 | bytes 7525720 | solution.py:171
  101.0 19.7 %custom-call.10 = f32[4,1,64,64]{2,3,1,0:T(8,128)S(1)} custom-call(f32[4,1,64,64]{3,2,1,0:T(8,128)S(1)} %fusion.178), custom_call_target="InvertDiagBlocksLowerTriangular" | custom-call | tf_op jit(solution)/shard_map/while/body/eval_jaxpr/jit(_solve_triangular)/vmap()/triangular_solve | solution.py:48
  134.2 19.7 %custom-call.10 = f32[4,1,64,64]{2,3,1,0:T(8,128)S(1)} custom-call(f32[4,1,64,64]{3,2,1,0:T(8,128)S(1)} %fusion.178), custom_call_target="InvertDiagBlocksLowerTriangular" | custom-call | tf_op jit(solution)/shard_map/while/body/eval_jaxpr/jit(_solve_triangular)/vmap()/triangular_solve | solution.py:48
  167.3 19.7 %custom-call.10 = f32[4,1,64,64]{2,3,1,0:T(8,128)S(1)} custom-call(f32[4,1,64,64]{3,2,1,0:T(8,128)S(1)} %fusion.178), custom_call_target="InvertDiagBlocksLowerTriangular" | custom-call | tf_op jit(solution)/shard_map/while/body/eval_jaxpr/jit(_solve_triangular)/vmap()/triangular_solve | solution.py:48
  200.5 19.7 %custom-call.10 = f32[4,1,64,64]{2,3,1,0:T(8,128)S(1)} custom-call(f32[4,1,64,64]{3,2,1,0:T(8,128)S(1)} %fusion.178), custom_call_target="InvertDiagBlocksLowerTriangular" | custom-call | tf_op jit(solution)/shard_map/while/body/eval_jaxpr/jit(_solve_triangular)/vmap()/triangular_solve | solution.py:48
  233.6 19.7 %custom-call.10 = f32[4,1,64,64]{2,3,1,0:T(8,128)S(1)} custom-call(f32[4,1,64,64]{3,2,1,0:T(8,128)S(1)} %fusion.178), custom_call_target="InvertDiagBlocksLowerTriangular" | custom-call | tf_op jit(solution)/shard_map/while/body/eval_jaxpr/jit(_solve_triangular)/vmap()/triangular_solve | solution.py:48
  266.8 19.7 %custom-call.10 = f32[4,1,64,64]{2,3,1,0:T(8,128)S(1)} custom-call(f32[4,1,64,64]{3,2,1,0:T(8,128)S(1)} %fusion.178), custom_call_target="InvertDiagBlocksLowerTriangular" | custom-call | tf_op jit(solution)/shard_map/while/body/eval_jaxpr/jit(_solve_triangular)/vmap()/triangular_solve | solution.py:48
  300.0 19.7 %custom-call.10 = f32[4,1,64,64]{2,3,1,0:T(8,128)S(1)} custom-call(f32[4,1,64,64]{3,2,1,0:T(8,128)S(1)} %fusion.178), custom_call_target="InvertDiagBlocksLowerTriangular" | custom-call | tf_op jit(solution)/shard_map/while/body/eval_jaxpr/jit(_solve_triangular)/vmap()/triangular_solve | solution.py:48
  333.1 19.7 %custom-call.10 = f32[4,1,64,64]{2,3,1,0:T(8,128)S(1)} custom-call(f32[4,1,64,64]{3,2,1,0:T(8,128)S(1)} %fusion.178), custom_call_target="InvertDiagBlocksLowerTriangular" | custom-call | tf_op jit(solution)/shard_map/while/body/eval_jaxpr/jit(_solve_triangular)/vmap()/triangular_solve | solution.py:48
  366.2 19.7 %custom-call.10 = f32[4,1,64,64]{2,3,1,0:T(8,128)S(1)} custom-call(f32[4,1,64,64]{3,2,1,0:T(8,128)S(1)} %fusion.178), custom_call_target="InvertDiagBlocksLowerTriangular" | custom-call | tf_op jit(solution)/shard_map/while/body/eval_jaxpr/jit(_solve_triangular)/vmap()/triangular_solve | solution.py:48
  399.4 19.7 %custom-call.10 = f32[4,1,64,64]{2,3,1,0:T(8,128)S(1)} custom-call(f32[4,1,64,64]{3,2,1,0:T(8,128)S(1)} %fusion.178), custom_call_target="InvertDiagBlocksLowerTriangular" | custom-call | tf_op jit(solution)/shard_map/while/body/eval_jaxpr/jit(_solve_triangular)/vmap()/triangular_solve | solution.py:48
  432.5 19.7 %custom-call.10 = f32[4,1,64,64]{2,3,1,0:T(8,128)S(1)} custom-call(f32[4,1,64,64]{3,2,1,0:T(8,128)S(1)} %fusion.178), custom_call_target="InvertDiagBlocksLowerTriangular" | custom-call | tf_op jit(solution)/shard_map/while/body/eval_jaxpr/jit(_solve_triangular)/vmap()/triangular_solve | solution.py:48
  465.7 19.7 %custom-call.10 = f32[4,1,64,64]{2,3,1,0:T(8,128)S(1)} custom-call(f32[4,1,64,64]{3,2,1,0:T(8,128)S(1)} %fusion.178), custom_call_target="InvertDiagBlocksLowerTriangular" | custom-call | tf_op jit(solution)/shard_map/while/body/eval_jaxpr/jit(_solve_triangular)/vmap()/triangular_solve | solution.py:48
  498.9 19.7 %custom-call.10 = f32[4,1,64,64]{2,3,1,0:T(8,128)S(1)} custom-call(f32[4,1,64,64]{3,2,1,0:T(8,128)S(1)} %fusion.178), custom_call_target="InvertDiagBlocksLowerTriangular" | custom-call | tf_op jit(solution)/shard_map/while/body/eval_jaxpr/jit(_solve_triangular)/vmap()/triangular_solve | solution.py:48
  532.0 19.7 %custom-call.10 = f32[4,1,64,64]{2,3,1,0:T(8,128)S(1)} custom-call(f32[4,1,64,64]{3,2,1,0:T(8,128)S(1)} %fusion.178), custom_call_target="InvertDiagBlocksLowerTriangular" | custom-call | tf_op jit(solution)/shard_map/while/body/eval_jaxpr/jit(_solve_triangular)/vmap()/triangular_solve | solution.py:48
  565.1 19.7 %custom-call.10 = f32[4,1,64,64]{2,3,1,0:T(8,128)S(1)} custom-call(f32[4,1,64,64]{3,2,1,0:T(8,128)S(1)} %fusion.178), custom_call_target="InvertDiagBlocksLowerTriangular" | custom-call | tf_op jit(solution)/shard_map/while/body/eval_jaxpr/jit(_solve_triangular)/vmap()/triangular_solve | solution.py:48
  598.2 19.7 %custom-call.10 = f32[4,1,64,64]{2,3,1,0:T(8,128)S(1)} custom-call(f32[4,1,64,64]{3,2,1,0:T(8,128)S(1)} %fusion.178), custom_call_target="InvertDiagBlocksLowerTriangular" | custom-call | tf_op jit(solution)/shard_map/while/body/eval_jaxpr/jit(_solve_triangular)/vmap()/triangular_solve | solution.py:48
  628.6 130.6 %while.29 = (s32[]{:T(128)}, f32[4,128,128]{2,1,0:T(8,128)S(1)}, f32[4,128,128]{2,1,0:T(8,128)S(1)}, f32[4,128,128]{2,1,0:T(8,128)S(1)}, s32[]{:T(128)}, /*index=5*/s32[]{:T(128)}) while((s32[]{:T(128)}, f32[4,128,128]{2,1,0:T(8,128)S(1)}, f32[4,128,128]{2,1,0:T(8,128)S(1)}, f32[4,128,128]{2,1,0:T(8,128)S(1)}, s32[]{:T(128)}, ...), condition=%wide.region_9.10_spmd.clone, body=%wide.region_8.9_spmd.clone.sunk | while | flops 100925440 | bytes 1835127 | solution.py:179
  629.0 3.4 collective-permute-start
  632.4 2.9 collective-permute-done
  635.7 4.4 collective-permute-start
  643.1 4.4 collective-permute-start
  650.4 4.4 collective-permute-start
  657.7 4.4 collective-permute-start
  665.0 5.3 collective-permute-start
  673.2 6.5 collective-permute-start
  682.6 6.6 collective-permute-start
  689.2 3.5 collective-permute-done
  693.1 7.1 collective-permute-start
  700.2 3.2 collective-permute-done
  703.8 6.3 collective-permute-start
  713.1 5.9 collective-permute-start
  721.9 6.5 collective-permute-start
  731.4 6.5 collective-permute-start
  740.8 6.5 collective-permute-start
  750.2 6.5 collective-permute-start
  759.2 5.5 multiply_reduce_fusion
  764.9 4.4 copy.60
  771.5 10.7 %convolution_convert_fusion = bf16[1024,2048]{1,0:T(8,128)(2,1)} fusion(bf16[512,2048]{1,0:T(8,128)(2,1)S(1)} %copy-done, f32[128,8,4,128]{3,2,1,0:T(4,128)} %bitcast.185, f32[128,8,4,128]{3,2,1,0:T(4,128)} %bitcast.187, bf16[1024,2048]{1,0:T(8,128)(2,1)} %all-gather.2.cloned.1.call-done, bf16[2048,512]{1,0:T(8,128)(2,1)} %param.23, f32[512]{0:T(512)S(1)} %copy-done.21), kind=kOutput, calls=%fused_computation.79 | convolution fusion | flops 4302307328 | bytes 16779264 | tf_op jit(solution)/shard_map/dot_general | solution.py:195
  782.3 49.4 %reduce-scatter.2.cloned.1.call-done = bf16[1024,256]{1,0:T(8,128)(2,1)} async-done(((bf16[1024,2048]{1,0:T(8,128)(2,1)}), bf16[1024,256]{1,0:T(8,128)(2,1)}) %reduce-scatter.2.cloned.1.call-update) | async-done | bytes 524304 | tf_op jit(solution)/shard_map/reduce_scatter | solution.py:196
  (609 shorter events, 286.0 us)
Async XLA Ops:
  6.5 765.0 %copy-start = (bf16[512,2048]{1,0:T(8,128)(2,1)S(1)}, bf16[512,2048]{1,0:T(8,128)(2,1)}, u32[]{:S(2)}) copy-start(bf16[512,2048]{1,0:T(8,128)(2,1)} %param.32) | copy-start | bytes 6291460
  6.5 40.7 %all-gather.2.cloned.1.call-start = ((), (), s32[]{:S(2)}) async-start(), calls=%async_computation.1 | async-start | bytes 4718592 | tf_op jit(solution)/shard_map/all_gather | solution.py:114
  7.3 824.4 %reduce-scatter.2.cloned.1.call-start = ((), (), s32[]{:S(2)}) async-start(), calls=%async_computation.2 | async-start | bytes 4718592 | tf_op jit(solution)/shard_map/reduce_scatter | solution.py:196
  47.3 5.4 copy-start.1
  47.3 5.4 copy-start.23
  52.6 1.3 copy-start.5
  52.6 1.6 copy-start.24
  53.9 1.6 copy-start.7
  54.2 5.7 copy-start.9
  54.2 5.7 copy-start.22
  55.5 0.8 copy-start.8
  56.3 4.9 copy-start.10
  56.3 9.0 %collective-permute-start.1 = (bf16[3,1024]{1,0:T(4,128)(2,1)S(1)}, bf16[3,1024]{1,0:T(4,128)(2,1)S(1)}, u32[]{:S(2)}, u32[]{:S(2)}) collective-permute-start(bf16[3,1024]{1,0:T(4,128)(2,1)S(1)} %pad_maximum_fusion), channel_id=1, source_target_pairs={{0,8},{8,16},{16,24},{24,32},{32,40},{40,48},{48,56},{56,64},{64,7... | collective-permute-start | bytes 18440 | tf_op jit(solution)/shard_map/ppermute | solution.py:19
  64.7 2.7 copy-start.17
  64.7 2.7 copy-start.18
  64.7 2.7 copy-start.19
  64.7 2.7 copy-start.20
  65.3 0.6 copy-start.11
  72.0 2.6 copy-start.3
  74.6 3.6 copy-start.13
  74.6 3.6 copy-start.14
  74.6 3.6 copy-start.15
  74.6 3.6 copy-start.16
  83.0 2.5 copy-start.12
  83.0 2.5 copy-start.6
  91.7 3.4 copy-start.4
  98.0 530.6 %copy-start.2 = (f32[4,128,128]{2,1,0:T(8,128)S(1)}, f32[4,128,128]{2,1,0:T(8,128)}, u32[]{:S(2)}) copy-start(f32[4,128,128]{2,1,0:T(8,128)} %custom-call.5) | copy-start | bytes 786436
  629.0 6.3 collective-permute-start
  635.7 6.9 collective-permute-start
  643.1 6.9 collective-permute-start
  650.4 6.9 collective-permute-start
  657.7 6.9 collective-permute-start
  665.0 7.8 collective-permute-start
  673.2 9.0 %collective-permute-start = (bf16[4,128,128]{2,1,0:T(8,128)(2,1)S(1)}, bf16[4,128,128]{2,1,0:T(8,128)(2,1)S(1)}, u32[]{:S(2)}, u32[]{:S(2)}) collective-permute-start(bf16[4,128,128]{2,1,0:T(8,128)(2,1)S(1)} %fusion.187), channel_id=1, source_target_pairs={{0,8},{8,16},{16,24},{24,32},{32,40},{40,48},{48,56},{56,64},{64,7... | collective-permute-start | bytes 393224 | tf_op jit(solution)/shard_map/while/body/eval_jaxpr/ppermute | solution.py:19
  682.6 10.1 %collective-permute-start = (bf16[4,128,128]{2,1,0:T(8,128)(2,1)S(1)}, bf16[4,128,128]{2,1,0:T(8,128)(2,1)S(1)}, u32[]{:S(2)}, u32[]{:S(2)}) collective-permute-start(bf16[4,128,128]{2,1,0:T(8,128)(2,1)S(1)} %fusion.187), channel_id=1, source_target_pairs={{0,8},{8,16},{16,24},{24,32},{32,40},{40,48},{48,56},{56,64},{64,7... | collective-permute-start | bytes 393224 | tf_op jit(solution)/shard_map/while/body/eval_jaxpr/ppermute | solution.py:19
  693.1 10.3 %collective-permute-start = (bf16[4,128,128]{2,1,0:T(8,128)(2,1)S(1)}, bf16[4,128,128]{2,1,0:T(8,128)(2,1)S(1)}, u32[]{:S(2)}, u32[]{:S(2)}) collective-permute-start(bf16[4,128,128]{2,1,0:T(8,128)(2,1)S(1)} %fusion.187), channel_id=1, source_target_pairs={{0,8},{8,16},{16,24},{24,32},{32,40},{40,48},{48,56},{56,64},{64,7... | collective-permute-start | bytes 393224 | tf_op jit(solution)/shard_map/while/body/eval_jaxpr/ppermute | solution.py:19
  703.8 8.8 %collective-permute-start = (bf16[4,128,128]{2,1,0:T(8,128)(2,1)S(1)}, bf16[4,128,128]{2,1,0:T(8,128)(2,1)S(1)}, u32[]{:S(2)}, u32[]{:S(2)}) collective-permute-start(bf16[4,128,128]{2,1,0:T(8,128)(2,1)S(1)} %fusion.187), channel_id=1, source_target_pairs={{0,8},{8,16},{16,24},{24,32},{32,40},{40,48},{48,56},{56,64},{64,7... | collective-permute-start | bytes 393224 | tf_op jit(solution)/shard_map/while/body/eval_jaxpr/ppermute | solution.py:19
  713.1 8.4 %collective-permute-start = (bf16[4,128,128]{2,1,0:T(8,128)(2,1)S(1)}, bf16[4,128,128]{2,1,0:T(8,128)(2,1)S(1)}, u32[]{:S(2)}, u32[]{:S(2)}) collective-permute-start(bf16[4,128,128]{2,1,0:T(8,128)(2,1)S(1)} %fusion.187), channel_id=1, source_target_pairs={{0,8},{8,16},{16,24},{24,32},{32,40},{40,48},{48,56},{56,64},{64,7... | collective-permute-start | bytes 393224 | tf_op jit(solution)/shard_map/while/body/eval_jaxpr/ppermute | solution.py:19
  721.9 9.0 %collective-permute-start = (bf16[4,128,128]{2,1,0:T(8,128)(2,1)S(1)}, bf16[4,128,128]{2,1,0:T(8,128)(2,1)S(1)}, u32[]{:S(2)}, u32[]{:S(2)}) collective-permute-start(bf16[4,128,128]{2,1,0:T(8,128)(2,1)S(1)} %fusion.187), channel_id=1, source_target_pairs={{0,8},{8,16},{16,24},{24,32},{32,40},{40,48},{48,56},{56,64},{64,7... | collective-permute-start | bytes 393224 | tf_op jit(solution)/shard_map/while/body/eval_jaxpr/ppermute | solution.py:19
  731.4 9.0 %collective-permute-start = (bf16[4,128,128]{2,1,0:T(8,128)(2,1)S(1)}, bf16[4,128,128]{2,1,0:T(8,128)(2,1)S(1)}, u32[]{:S(2)}, u32[]{:S(2)}) collective-permute-start(bf16[4,128,128]{2,1,0:T(8,128)(2,1)S(1)} %fusion.187), channel_id=1, source_target_pairs={{0,8},{8,16},{16,24},{24,32},{32,40},{40,48},{48,56},{56,64},{64,7... | collective-permute-start | bytes 393224 | tf_op jit(solution)/shard_map/while/body/eval_jaxpr/ppermute | solution.py:19
  740.8 9.0 %collective-permute-start = (bf16[4,128,128]{2,1,0:T(8,128)(2,1)S(1)}, bf16[4,128,128]{2,1,0:T(8,128)(2,1)S(1)}, u32[]{:S(2)}, u32[]{:S(2)}) collective-permute-start(bf16[4,128,128]{2,1,0:T(8,128)(2,1)S(1)} %fusion.187), channel_id=1, source_target_pairs={{0,8},{8,16},{16,24},{24,32},{32,40},{40,48},{48,56},{56,64},{64,7... | collective-permute-start | bytes 393224 | tf_op jit(solution)/shard_map/while/body/eval_jaxpr/ppermute | solution.py:19
  750.2 9.0 %collective-permute-start = (bf16[4,128,128]{2,1,0:T(8,128)(2,1)S(1)}, bf16[4,128,128]{2,1,0:T(8,128)(2,1)S(1)}, u32[]{:S(2)}, u32[]{:S(2)}) collective-permute-start(bf16[4,128,128]{2,1,0:T(8,128)(2,1)S(1)} %fusion.187), channel_id=1, source_target_pairs={{0,8},{8,16},{16,24},{24,32},{32,40},{40,48},{48,56},{56,64},{64,7... | collective-permute-start | bytes 393224 | tf_op jit(solution)/shard_map/while/body/eval_jaxpr/ppermute | solution.py:19
  769.3 2.2 copy-start.21
Sparse Core Ops, SparseCore 0:
  9.0 38.2 all-gather.1
  782.4 49.1 reduce-scatter.1
where the time goes:
time: 842 us; the launch traced here: 839 us
  other arithmetic  378 us (45%)
  matrix products  202 us (24%)
  waiting for transfers between devices  122 us (14%)
  starting transfers between devices  88 us (10%)
  local copies, waits for them, and re-layouts  30.7 us (4%)
  between operations  13.9 us (2%)
    another operation x48, other arithmetic, block_terms(): jax.scipy.linalg.solve_triangular(system, right_hand, lower=True, unit_di...  315 us
    dot_general x176, matrix products, composed_product(): return jnp.einsum(form, left_side, right_side, precision=highest)  172 us
    ppermute x16, starting transfers between devices, passed_along(): return lax.ppermute(array, axis, pairs)  88 us
    reduce_scatter x1, waiting for transfers between devices, per_device(): lax.psum_scatter(partial_sum.astype(jnp.bfloat16), 'head', scatter_dimens...  49.4 us
    ppermute x16, waiting for transfers between devices, passed_along(): return lax.ppermute(array, axis, pairs)  39.5 us
    all_gather x1, waiting for transfers between devices, per_device(): columns_in = lax.all_gather(hidden_in, 'head', axis=1, tiled=True)  32.7 us
    mul x16, other arithmetic, block_terms(): (betas * scaled)[:, :, None] * keys_in  17.9 us
  transfers between devices with their start and end apart: 18, of which 17 were waited for; matrix products, arithmetic and copies ran while one was open for 2% of the time, Pallas kernels for 0%

commit v1 on v0

v1 whole, which is shorter than its diff:
```python
import functools
import jax
import jax.numpy as jnp
from jax import lax
from jax.experimental import pallas as pl
from jax.experimental.pallas import tpu as pltpu
BLOCK = 64
GROUP = 4
ROWS = BLOCK * GROUP
HD = 128
f32 = jnp.float32
bf16 = jnp.bfloat16

def dotf(a, b):
    return jnp.dot(a, b, preferred_element_type=f32)

def split2(x):
    hi = x.astype(bf16)
    return hi, (x - hi.astype(f32)).astype(bf16)

def sigmoid(x):
    return 1.0 / (1.0 + jnp.exp(-x))

def local_kernel(info, q_ref, k_ref, v_ref, halo_ref, ba_ref, dec_ref, taps_ref,
                 out_ref, lift_ref, st_ref, carry):
    step = pl.program_id(0)

    @pl.when(step == 0)
    def _():
        rows = lax.broadcasted_iota(jnp.int32, (HD, 2 * HD), 0)
        cols = lax.broadcasted_iota(jnp.int32, (HD, 2 * HD), 1)
        init = jnp.where(cols - HD == rows, 1.0, 0.0).astype(f32)
        for h in range(4):
            st_ref[h] = init
        carry[...] = halo_ref[...]

    base = info[0] + step * ROWS
    pos = base + lax.broadcasted_iota(jnp.int32, (ROWS, HD), 0)
    start = jnp.zeros((ROWS, HD), jnp.int32)
    off = info[1] * 0
    for n in range(6):
        start = jnp.maximum(start, jnp.where(pos >= off, off, 0))
        off = off + info[1 + n]
    rel = pos - start
    keep = [None, rel >= 1, rel >= 2, rel >= 3]

    def conv(ref, c, w):
        x0 = ref[:, c * HD:(c + 1) * HD].astype(f32)
        x = jnp.concatenate([carry[:, w * HD:(w + 1) * HD], x0], axis=0)
        carry[:, w * HD:(w + 1) * HD] = x0[ROWS - 8:]
        y = taps_ref[3:4, w * HD:(w + 1) * HD] * x0
        for lag in (1, 2, 3):
            t = taps_ref[3 - lag:4 - lag, w * HD:(w + 1) * HD]
            y = y + jnp.where(keep[lag], t * x[8 - lag:8 - lag + ROWS], 0.0)
        return y * sigmoid(y)

    def unit(x):
        return x * lax.rsqrt(jnp.sum(x * x, axis=-1, keepdims=True) + 1e-06)

    qs = [unit(conv(q_ref, c, c)) * HD ** (-0.5) for c in range(2)]
    ks = [unit(conv(k_ref, c, 2 + c)) for c in range(2)]
    vs = [conv(v_ref, c, 4 + c) for c in range(4)]
    qb = [x.astype(bf16) for x in qs]
    kb = [x.astype(bf16) for x in ks]
    ba = ba_ref[...]
    beta = sigmoid(ba)
    z = ba + dec_ref[0:1, :]
    g = dec_ref[1:2, :] * (jnp.maximum(z, 0.0) + jnp.log1p(jnp.exp(-jnp.abs(z))))

    ii = lax.broadcasted_iota(jnp.int32, (BLOCK, 256), 0)
    ll = lax.broadcasted_iota(jnp.int32, (BLOCK, 256), 1)
    jl = ll & (BLOCK - 1)
    xor = ii ^ jl
    head_of = ll >> 6
    low = lax.broadcasted_iota(jnp.int32, (BLOCK, HD), 1) < BLOCK
    ltri = jnp.where(
        lax.broadcasted_iota(jnp.int32, (BLOCK, BLOCK), 0)
        >= lax.broadcasted_iota(jnp.int32, (BLOCK, BLOCK), 1), 1.0, 0.0).astype(f32)
    hmask = [head_of == r for r in range(4)]

    def bd(m):
        z = jnp.zeros_like(m)
        return jnp.concatenate([jnp.where(hmask[r], m, z) for r in range(4)], axis=0)

    def packed(x, first, r):
        cols = [x[r, first + h:first + h + 1] for h in range(4)]
        return jnp.concatenate(
            [jnp.where(low, cols[0], cols[1]), jnp.where(low, cols[2], cols[3])], axis=1)

    def bdh(m):
        return bd(m).astype(bf16)

    def mul3(x, m):
        xh, xl = split2(x)
        mh = m.astype(bf16).astype(f32)
        ml = m - mh
        y = dotf(jnp.concatenate([xh, xl], axis=0), bdh(mh))
        return y[:BLOCK] + y[BLOCK:] + dotf(xh, bdh(ml))

    def mul1(x, m):
        return dotf(x.astype(bf16), bdh(m))

    blocks = range(GROUP)
    rs = [slice(b * BLOCK, (b + 1) * BLOCK) for b in blocks]
    L, A, spreads = [], [], []
    for b in blocks:
        r = rs[b]
        gm = jnp.where(ii > jl, packed(g, 4, r), 0.0)
        spread = jnp.dot(ltri, gm, precision=lax.Precision.HIGHEST, preferred_element_type=f32)
        spreads.append(spread)
        st2 = jnp.concatenate([start[r], start[r]], axis=1)
        mask = (ii >= jl) & (base + b * BLOCK + jl >= st2)
        factor = jnp.where(mask, jnp.exp(jnp.minimum(spread, 0.0)), 0.0)
        gr = []
        for c in range(2):
            kk = kb[c][r]
            gr.append(lax.dot_general(
                jnp.concatenate([kk, qb[c][r]], axis=0), jnp.concatenate([kk, kk], axis=0),
                (((1,), (1,)), ((), ())), preferred_element_type=f32))
        both = jnp.concatenate(gr, axis=1)
        L.append(jnp.where(ii > jl, packed(beta, 0, r) * factor * both[:BLOCK], 0.0))
        A.append(factor * both[BLOCK:])
    eye = jnp.where(xor == 0, 1.0, 0.0).astype(f32)
    X = [eye - jnp.where(xor == 1, L[b], 0.0) for b in blocks]
    for m in (2, 4, 8, 16, 32):
        level = (xor >= m) & (xor < 2 * m)
        Y = [mul3(X[b], jnp.where(level, L[b], 0.0)) for b in blocks]
        X = [X[b] - mul3(Y[b], X[b]) for b in blocks]
    UW, AUW, scal, Kt, sd = [], [], [], [], []
    for b in blocks:
        r = rs[b]
        rows, sc, kt, dd = [], [], [], []
        for h in range(4):
            c = h // 2
            cum = spreads[b][:, h * BLOCK:h * BLOCK + 1] + g[b * BLOCK:b * BLOCK + 1, 4 + h:5 + h]
            alive = start[r] < base + b * BLOCK
            s = jnp.where(alive, jnp.exp(cum), 0.0)
            last = cum[BLOCK - 1:]
            tail_start = start[(b + 1) * BLOCK - 1:(b + 1) * BLOCK]
            tr = jnp.where(pos[r] >= tail_start, jnp.exp(jnp.minimum(last - cum, 0.0)), 0.0)
            bt = beta[r, h:h + 1]
            rows.append(jnp.concatenate([bt * vs[h][r], bt * s * ks[c][r]], axis=1).astype(bf16))
            sc.append(s)
            kt.append(jnp.transpose(tr * ks[c][r]).astype(bf16))
            dd.append(s[BLOCK - 1:])
        UW.append(dotf(bdh(X[b]), jnp.concatenate(rows, axis=0)))
        scal.append(sc)
        Kt.append(kt)
        sd.append(dd)
    for b in blocks:
        AUW.append(dotf(bdh(A[b]), UW[b].astype(bf16)))
    state = [st_ref[h] for h in range(4)]
    for b in blocks:
        r = rs[b]
        for h in range(4):
            c = h // 2
            hr = slice(h * BLOCK, (h + 1) * BLOCK)
            P = scal[b][h] * qs[c][r] - AUW[b][hr, HD:]
            zp = jnp.concatenate([UW[b][hr, HD:].astype(bf16), P.astype(bf16)], axis=0)
            res = dotf(zp, state[h].astype(bf16))
            out_ref[r, h * HD:(h + 1) * HD] = AUW[b][hr, :HD] + res[BLOCK:, :HD]
            lift_ref[r, h * HD:(h + 1) * HD] = res[BLOCK:, HD:].astype(bf16)
            D = jnp.concatenate([UW[b][hr, :HD] - res[:BLOCK, :HD], -res[:BLOCK, HD:]], axis=1)
            dec = jnp.concatenate([sd[b][h], sd[b][h]], axis=1)
            state[h] = dec * state[h] + dotf(Kt[b][h], D.astype(bf16))
    for h in range(4):
        st_ref[h] = state[h]

def local_scan(info, q, k, v, halo, ba, dec, taps):
    n = q.shape[0]
    row = lambda w: pl.BlockSpec((ROWS, w), lambda i: (i, 0))
    whole = lambda s: pl.BlockSpec(s, lambda i: (0,) * len(s))
    return pl.pallas_call(
        local_kernel,
        grid=(n // ROWS,),
        in_specs=[pl.BlockSpec(memory_space=pltpu.SMEM), row(256), row(256), row(512),
                  whole((8, 1024)), row(8), whole((2, 8)), whole((4, 1024))],
        out_specs=[row(512), row(512), whole((4, HD, 2 * HD))],
        out_shape=[jax.ShapeDtypeStruct((n, 512), f32), jax.ShapeDtypeStruct((n, 512), bf16),
                   jax.ShapeDtypeStruct((4, HD, 2 * HD), f32)],
        scratch_shapes=[pltpu.VMEM((8, 1024), f32)],
        name="local_scan",
    )(info, q, k, v, halo, ba, dec, taps)
from jax.sharding import PartitionSpec as P

MESH = pl.DeviceIdType.MESH
TURNS = 8
SEQ = 16


def chain_kernel(t_ref, b_ref, in_ref, sent, held, send_sem, recv_sem):
    s = lax.axis_index("seq")
    after = lax.rem(s + 1, SEQ)
    barrier = pltpu.get_barrier_semaphore()
    pl.semaphore_signal(
        barrier, inc=1, device_id={"seq": lax.rem(s + SEQ - 1, SEQ)}, device_id_type=MESH)
    pl.semaphore_wait(barrier, 1)

    def hop(t, h):
        return pltpu.make_async_remote_copy(
            src_ref=sent.at[t, h], dst_ref=held.at[t, h], send_sem=send_sem.at[t, h],
            recv_sem=recv_sem.at[t, h], device_id={"seq": after}, device_id_type=MESH)

    for h in range(4):
        sent[0, h] = b_ref[h].astype(bf16)
        hop(0, h).start()

    def turn(t, carry):
        for h in range(4):
            hop(t - 1, h).wait_recv()
            arrived = held[t - 1, h]
            hi, lo = split2(t_ref[h])
            out = dotf(jnp.concatenate([hi, lo], axis=1),
                       jnp.concatenate([arrived, arrived], axis=0)) + b_ref[h]
            sent[t, h] = out.astype(bf16)
            hop(t, h).start()
        return carry

    lax.fori_loop(1, TURNS, turn, 0)
    for h in range(4):
        hop(TURNS - 1, h).wait_recv()
        in_ref[h] = held[TURNS - 1, h]

    def drain(t, carry):
        for h in range(4):
            hop(t, h).wait_send()
        return carry

    lax.fori_loop(0, TURNS, drain, 0)


def hand_over(across, local_state):
    vm = pl.BlockSpec(memory_space=pltpu.VMEM)
    return pl.pallas_call(
        chain_kernel,
        in_specs=[vm, vm], out_specs=vm,
        out_shape=jax.ShapeDtypeStruct((4, HD, HD), bf16),
        scratch_shapes=[pltpu.VMEM((TURNS, 4, HD, HD), bf16), pltpu.VMEM((TURNS, 4, HD, HD), bf16),
                        pltpu.SemaphoreType.DMA((TURNS, 4)), pltpu.SemaphoreType.DMA((TURNS, 4))],
        compiler_params=pltpu.CompilerParams(collective_id=1, has_side_effects=True),
        name="hand_over",
    )(across, local_state)


def gated_rows(o_ref, l_ref, s_ref, z_ref, nw_ref, r):
    cols = []
    for h in range(4):
        c = slice(h * HD, (h + 1) * HD)
        o = o_ref[r, c] + dotf(l_ref[r, c], s_ref[h])
        var = jnp.mean(o * o, axis=-1, keepdims=True)
        z = z_ref[r, c].astype(f32)
        cols.append((o * lax.rsqrt(var + 1e-06) * nw_ref[...] * (z * sigmoid(z))).astype(bf16))
    return jnp.concatenate(cols, axis=1)


def out_kernel(o_ref, l_ref, s_ref, z_ref, nw_ref, w_ref, p_ref):
    normed = gated_rows(o_ref, l_ref, s_ref, z_ref, nw_ref, slice(None))
    p_ref[...] = dotf(normed, w_ref[...]).astype(bf16)


def out_share(o, lift, s_in, z, nw, w):
    n = o.shape[0]
    row = lambda w: pl.BlockSpec((ROWS, w), lambda i: (i, 0))
    whole = lambda s: pl.BlockSpec(s, lambda i: (0,) * len(s))
    return pl.pallas_call(
        out_kernel, grid=(n // ROWS,),
        in_specs=[row(512), row(512), whole((4, HD, HD)), row(512), whole((1, HD)), whole((512, 2048))],
        out_specs=row(2048), out_shape=jax.ShapeDtypeStruct((n, 2048), bf16), name="out_share",
    )(o, lift, s_in, z, nw, w)


def per_device(hidden_in, w_query, w_key, w_value, w_gate, w_beta, w_alpha, dt_bias, head_decay,
               conv_query, conv_key, conv_value, norm_weight, w_out, prompt_lengths):
    n = hidden_in.shape[0]
    columns_in = lax.all_gather(hidden_in, "head", axis=1, tiled=True)
    q, k, v, z = (dotf(columns_in, w).astype(bf16) for w in (w_query, w_key, w_value, w_gate))
    ba = dotf(columns_in, jnp.concatenate([w_beta, w_alpha], axis=1))
    tails = jnp.concatenate([q[n - 8:], k[n - 8:], v[n - 8:]], axis=1)
    halo = lax.ppermute(tails, "seq", [(i, i + 1) for i in range(SEQ - 1)]).astype(f32)
    info = jnp.concatenate([jnp.reshape(lax.axis_index("seq") * n, (1,)), prompt_lengths]).astype(jnp.int32)
    zero4 = jnp.zeros((4,), f32)
    dec = jnp.stack([jnp.concatenate([zero4, dt_bias]), jnp.concatenate([zero4, -head_decay])])
    taps = jnp.concatenate([conv_query, conv_key, conv_value], axis=1).astype(f32)
    o, lift, st = local_scan(info, q, k, v, halo, ba, dec, taps)
    s_in = hand_over(st[:, :, HD:], st[:, :, :HD])
    part = out_share(o, lift, s_in, z, norm_weight[None, :], w_out)
    return lax.psum_scatter(part, "head", scatter_dimension=1, tiled=True)


def solution(mesh):
    rows, cols = P("seq", "head"), P(None, "head")
    in_specs = (rows, cols, cols, cols, cols, cols, cols, P("head"), P("head"), cols, cols, cols,
                P(), P("head", None), P())
    return jax.shard_map(per_device, mesh=mesh, in_specs=in_specs, out_specs=rows, check_vma=False)
```

time: 842 us -> 176 us (0.21)
  other arithmetic: 378 us -> 4.34 us
  matrix products: 202 us -> 12.8 us
  starting transfers between devices: 88 us -> 3.74 us
  Pallas kernels: 0 us -> 64.4 us
  waiting for transfers between devices: 122 us -> 73.4 us
  local copies, waits for them, and re-layouts: 30.7 us -> 3.44 us
    another operation x99 -> x1, other arithmetic: 323 us -> 0.52 us  [per_device(): jnp.stack([jnp.concatenate([zero4, dt_bias]), jnp.concatenate([zero4, -he...]
    dot_general x182 -> x5, matrix products: 195 us -> 12.8 us  [dotf(): return jnp.dot(a, b, preferred_element_type=f32)]
    ppermute x16 -> x1, starting transfers between devices: 88 us -> 3.7 us  [per_device(): lax.ppermute(tails, 'seq', [(i, i + 1) for i in range(SEQ - 1)]).astype(f32)]
    pallas_call x0 -> x3, Pallas kernels: none -> 64.4 us  [the longest x1 35 us: hand_over(): pl.pallas_call(chain_kernel, in_specs=[vm, vm], out_specs=vm, out_shape=j...]
    mul x40 -> x0, other arithmetic: 43.6 us -> none  [the longest x16 17.9 us: block_terms(): (betas * scaled)[:, :, None] * keys_in]
    ppermute x16 -> x1, waiting for transfers between devices: 39.5 us -> 0.01 us  [per_device(): lax.ppermute(tails, 'seq', [(i, i + 1) for i in range(SEQ - 1)]).astype(f32)]
    reduce_scatter x1, waiting for transfers between devices: 49.4 us -> 37.2 us  [per_device(): return lax.psum_scatter(part, 'head', scatter_dimension=1, tiled=True)]
  transfers between devices with their start and end apart: 18 -> 3, of which waited for: 17 -> 2; matrix products, arithmetic and copies ran while one was open for 2% -> 6% of each run, Pallas kernels for 0% -> 0%
where the time goes in v1:
time: 176 us
  waiting for transfers between devices  73.4 us (42%)
  Pallas kernels  64.4 us (37%)
  between operations  13.5 us (8%)
  matrix products  12.8 us (7%)
  other arithmetic  4.34 us (2%)
  starting transfers between devices  3.74 us (2%)
  local copies, waits for them, and re-layouts  3.44 us (2%)
    reduce_scatter x1, waiting for transfers between devices, per_device(): return lax.psum_scatter(part, 'head', scatter_dimension=1, tiled=True)  37.2 us
    all_gather x1, waiting for transfers between devices, per_device(): columns_in = lax.all_gather(hidden_in, 'head', axis=1, tiled=True)  35.5 us
    pallas_call x1, Pallas kernels, hand_over(): pl.pallas_call(chain_kernel, in_specs=[vm, vm], out_specs=vm, out_shape=j...  35 us
    pallas_call x1, Pallas kernels, local_scan(): pl.pallas_call(local_kernel, grid=(n // ROWS,), in_specs=[pl.BlockSpec(me...  21.5 us
    dot_general x5, matrix products, dotf(): return jnp.dot(a, b, preferred_element_type=f32)  12.8 us
    pallas_call x1, Pallas kernels, out_share(): pl.pallas_call(out_kernel, grid=(n // ROWS,), in_specs=[row(512), row(512...  7.88 us
    ppermute x1, starting transfers between devices, per_device(): lax.ppermute(tails, 'seq', [(i, i + 1) for i in range(SEQ - 1)]).astype(f32)  3.7 us
  transfers between devices with their start and end apart: 3, of which 2 were waited for; matrix products, arithmetic and copies ran while one was open for 6% of the time, Pallas kernels for 0%

profile of v1, /device:TPU:0, one launch (start us, length us, event | category | flops | bytes accessed | tf_op | source)
XLA Modules:
  0.0 175.7 jit_solution(5141942979564397172)
XLA Ops:
  6.5 0.0 copy-start
  6.5 0.0 copy-start.6
  6.5 0.0 all-gather.2.cloned.1.call-start
  6.5 0.7 all-gather.2.cloned.1.call-update
  7.3 0.0 reduce-scatter.2.cloned.1.call-start
  7.3 0.7 neg.3
  8.0 1.2 pad_add_fusion.info
  9.2 0.7 pad_bitcast_fusion
  9.9 0.5 pad_maximum_fusion.1.dec_ref
  10.5 1.3 maximum_convert_fusion.taps_ref
  11.8 35.5 %all-gather.2.cloned.1.call-done = bf16[1024,2048]{1,0:T(8,128)(2,1)} async-done(((bf16[1024,256]{1,0:T(8,128)(2,1)}), bf16[1024,2048]{1,0:T(8,128)(2,1)}) %all-gather.2.cloned.1.call-update) | async-done | bytes 4194320 | tf_op jit(solution)/shard_map/all_gather | solution.py:275
  47.3 0.0 copy-start.4
  47.3 3.9 %convolution_convert_fusion.2.k_ref = bf16[1024,256]{1,0:T(8,128)(2,1)S(1)} fusion(bf16[1024,2048]{1,0:T(8,128)(2,1)} %all-gather.2.cloned.1.call-done, bf16[2048,256]{1,0:T(8,128)(2,1)} %param.17), kind=kOutput, calls=%fused_computation.2 | convolution fusion | flops 1074003968 | bytes 5767168 | tf_op jit(solution)/shard_map/dot_general | solution.py:15
  51.2 0.0 copy-start.2
  51.2 0.0 copy-done.6
  51.2 0.0 copy-done.4
  51.2 1.3 convolution_convert_fusion.3.q_ref
  52.5 0.0 copy-done.2
  52.5 0.0 copy-start.3
  52.5 0.8 copy-done.3
  53.3 0.0 copy-done
  53.3 0.0 copy-start.5
  53.3 2.3 %convolution_convert_fusion.1.v_ref = bf16[1024,512]{1,0:T(8,128)(2,1)S(1)} fusion(bf16[1024,2048]{1,0:T(8,128)(2,1)S(1)} %copy-done.4, bf16[2048,512]{1,0:T(8,128)(2,1)S(1)} %copy-done), kind=kOutput, calls=%fused_computation.1 | convolution fusion | flops 2148007936 | bytes 7340032 | tf_op jit(solution)/shard_map/dot_general | solution.py:15
  55.6 0.0 copy-start.1
  55.6 0.0 copy-start.7
  55.7 0.0 copy-start.8
  55.7 3.7 %collective-permute-start = (bf16[8,1024]{1,0:T(8,128)(2,1)S(1)}, bf16[8,1024]{1,0:T(8,128)(2,1)S(1)}, u32[]{:S(2)}, u32[]{:S(2)}) collective-permute-start(bf16[8,1024]{1,0:T(8,128)(2,1)S(1)} %pad_maximum_fusion), channel_id=1, source_target_pairs={{0,8},{8,16},{16,24},{24,32},{32,40},{40,48},{48,56},{56,64},{64,7... | collective-permute-start | bytes 49160 | tf_op jit(solution)/shard_map/ppermute | solution.py:279
  59.4 0.0 copy-done.5
  59.4 3.3 %convolution_convert_fusion.z_ref = bf16[1024,512]{1,0:T(8,128)(2,1)} fusion(bf16[1024,2048]{1,0:T(8,128)(2,1)S(1)} %copy-done.4, bf16[2048,512]{1,0:T(8,128)(2,1)S(1)} %copy-done.5), kind=kOutput, calls=%fused_computation | convolution fusion | flops 2148007936 | bytes 7340032 | tf_op jit(solution)/shard_map/dot_general | solution.py:15
  62.7 0.0 copy-done.1
  62.7 0.0 copy-done.7
  62.7 0.0 copy-done.8
  62.7 2.0 %convolution_bitcast_fusion.ba_ref = f32[1024,8]{1,0:T(8,128)} fusion(bf16[1024,2048]{1,0:T(8,128)(2,1)S(1)} %copy-done.4, bf16[2048,4]{0,1:T(4,128)(2,1)S(1)} %copy-done.7, bf16[2048,4]{0,1:T(4,128)(2,1)S(1)} %copy-done.8), kind=kOutput, calls=%fused_computation.4 | convolution fusion | flops 33619968 | bytes 4259840 | tf_op jit(solution)/shard_map/dot_general | solution.py:15
  64.7 0.0 collective-permute-done
  64.7 0.6 convert_element_type.21.halo_ref
  65.3 21.5 %local_scan.1 = (f32[1024,512]{1,0:T(8,128)}, bf16[1024,512]{1,0:T(8,128)(2,1)}, f32[4,128,256]{2,1,0:T(8,128)}) custom-call(s32[7]{0:T(128)} %pad_add_fusion.info, bf16[1024,256]{1,0:T(8,128)(2,1)} %copy-done.3, bf16[1024,256]{1,0:T(8,128)(2,1)} %copy-done.2, bf16[1024,512]{1,0:T(8,128)(2,1)} %copy-done.1, f32[8,1024]{1,0:T(8,128)} %convert_element_type.21.halo_ref, ...), custom_call_target="tpu_custom_call" | custom-call | tf_op jit(solution)/shard_map/local_scan/pallas_call | solution.py:173
  86.8 1.9 %fusion.4 = (f32[4,128,128]{2,1,0:T(8,128)}, f32[4,128,128]{2,1,0:T(8,128)}) fusion(f32[4,128,256]{2,1,0:T(8,128)} %get-tuple-element.10), kind=kLoop, calls=%fused_computation.15 | loop fusion | bytes 1048576 | tf_op jit(solution)/shard_map/slice | solution.py:285
  88.7 35.0 %hand_over.1.s_ref = bf16[4,128,128]{2,1,0:T(8,128)(2,1)} custom-call(f32[4,128,128]{2,1,0:T(8,128)} %get-tuple-element.12.t_ref, f32[4,128,128]{2,1,0:T(8,128)} %get-tuple-element.11.b_ref), custom_call_target="tpu_custom_call" | custom-call | tf_op jit(solution)/shard_map/hand_over/pallas_call | solution.py:234
  123.8 7.9 %out_share.1 = bf16[1024,2048]{1,0:T(8,128)(2,1)} custom-call(f32[1024,512]{1,0:T(8,128)} %get-tuple-element.8.o_ref, bf16[1024,512]{1,0:T(8,128)(2,1)} %get-tuple-element.9.l_ref, bf16[4,128,128]{2,1,0:T(8,128)(2,1)} %hand_over.1.s_ref, bf16[1024,512]{1,0:T(8,128)(2,1)} %convolution_convert_fusion.z_ref, f32[1,128]{1,0:T(1,128)} %bitcast.17, ...), custom_call_target="tpu_custom_call" | custom-call | tf_op jit(solution)/shard_map/out_share/pallas_call | solution.py:265
  131.6 0.0 reduce-scatter.2.cloned.1.call-update
  131.7 37.2 %reduce-scatter.2.cloned.1.call-done = bf16[1024,256]{1,0:T(8,128)(2,1)} async-done(((bf16[1024,2048]{1,0:T(8,128)(2,1)}), bf16[1024,256]{1,0:T(8,128)(2,1)}) %reduce-scatter.2.cloned.1.call-update) | async-done | bytes 524304 | tf_op jit(solution)/shard_map/reduce_scatter | solution.py:287
  (4 shorter events, 0.0 us)
Async XLA Ops:
  6.5 46.7 %copy-start = (bf16[2048,512]{1,0:T(8,128)(2,1)S(1)}, bf16[2048,512]{1,0:T(8,128)(2,1)}, u32[]{:S(2)}) copy-start(bf16[2048,512]{1,0:T(8,128)(2,1)} %param.18) | copy-start | bytes 6291460
  6.5 44.6 %copy-start.6 = (bf16[2048,256]{1,0:T(8,128)(2,1)S(1)}, bf16[2048,256]{1,0:T(8,128)(2,1)}, u32[]{:S(2)}) copy-start(bf16[2048,256]{1,0:T(8,128)(2,1)} %param.16) | copy-start | bytes 3145732
  6.5 40.7 %all-gather.2.cloned.1.call-start = ((), (), s32[]{:S(2)}) async-start(), calls=%async_computation.1 | async-start | bytes 4718592 | tf_op jit(solution)/shard_map/all_gather | solution.py:275
  7.3 161.6 %reduce-scatter.2.cloned.1.call-start = ((), (), s32[]{:S(2)}) async-start(), calls=%async_computation.2 | async-start | bytes 4718592 | tf_op jit(solution)/shard_map/reduce_scatter | solution.py:287
  47.3 3.9 %copy-start.4 = (bf16[1024,2048]{1,0:T(8,128)(2,1)S(1)}, bf16[1024,2048]{1,0:T(8,128)(2,1)}, u32[]{:S(2)}) copy-start(bf16[1024,2048]{1,0:T(8,128)(2,1)} %all-gather.2.cloned.1.call-done) | copy-start | bytes 12582916
  51.2 1.3 copy-start.2
  52.5 0.8 copy-start.3
  53.3 6.1 %copy-start.5 = (bf16[2048,512]{1,0:T(8,128)(2,1)S(1)}, bf16[2048,512]{1,0:T(8,128)(2,1)}, u32[]{:S(2)}) copy-start(bf16[2048,512]{1,0:T(8,128)(2,1)} %param.19) | copy-start | bytes 6291460
  55.6 7.1 %copy-start.1 = (bf16[1024,512]{1,0:T(8,128)(2,1)}, bf16[1024,512]{1,0:T(8,128)(2,1)S(1)}, u32[]{:S(2)}) copy-start(bf16[1024,512]{1,0:T(8,128)(2,1)S(1)} %convolution_convert_fusion.1.v_ref) | copy-start | bytes 3145732
  55.6 7.1 %copy-start.7 = (bf16[2048,4]{0,1:T(4,128)(2,1)S(1)}, bf16[2048,4]{0,1:T(4,128)(2,1)}, u32[]{:S(2)}) copy-start(bf16[2048,4]{0,1:T(4,128)(2,1)} %param.21) | copy-start | bytes 49156
  55.7 7.0 %copy-start.8 = (bf16[2048,4]{0,1:T(4,128)(2,1)S(1)}, bf16[2048,4]{0,1:T(4,128)(2,1)}, u32[]{:S(2)}) copy-start(bf16[2048,4]{0,1:T(4,128)(2,1)} %param.20) | copy-start | bytes 49156
  55.7 9.1 %collective-permute-start = (bf16[8,1024]{1,0:T(8,128)(2,1)S(1)}, bf16[8,1024]{1,0:T(8,128)(2,1)S(1)}, u32[]{:S(2)}, u32[]{:S(2)}) collective-permute-start(bf16[8,1024]{1,0:T(8,128)(2,1)S(1)} %pad_maximum_fusion), channel_id=1, source_target_pairs={{0,8},{8,16},{16,24},{24,32},{32,40},{40,48},{48,56},{56,64},{64,7... | collective-permute-start | bytes 49160 | tf_op jit(solution)/shard_map/ppermute | solution.py:279
Sparse Core Ops, SparseCore 0:
  9.0 38.2 all-gather.1
  131.8 37.0 reduce-scatter.1

commit v2 on v1

--- a/solution.py
+++ b/solution.py
@@ -21,7 +21,7 @@
 def sigmoid(x):
     return 1.0 / (1.0 + jnp.exp(-x))
 
-def local_kernel(info, q_ref, k_ref, v_ref, halo_ref, ba_ref, dec_ref, taps_ref,
+def local_kernel(lens, dt, decay, q_ref, k_ref, v_ref, halo_ref, ba_ref, tq_ref, tk_ref, tv_ref,
                  out_ref, lift_ref, st_ref, carry):
     step = pl.program_id(0)
 
@@ -32,40 +32,46 @@
         init = jnp.where(cols - HD == rows, 1.0, 0.0).astype(f32)
         for h in range(4):
             st_ref[h] = init
-        carry[...] = halo_ref[...]
-
-    base = info[0] + step * ROWS
+        carry[...] = halo_ref[8:].astype(f32)
+
+    base = (lax.axis_index("seq") * pl.num_programs(0) + step) * ROWS
     pos = base + lax.broadcasted_iota(jnp.int32, (ROWS, HD), 0)
     start = jnp.zeros((ROWS, HD), jnp.int32)
-    off = info[1] * 0
+    off = lens[0] * 0
     for n in range(6):
         start = jnp.maximum(start, jnp.where(pos >= off, off, 0))
-        off = off + info[1 + n]
+        off = off + lens[n]
     rel = pos - start
     keep = [None, rel >= 1, rel >= 2, rel >= 3]
 
-    def conv(ref, c, w):
+    def conv(ref, tap_ref, c, w):
         x0 = ref[:, c * HD:(c + 1) * HD].astype(f32)
         x = jnp.concatenate([carry[:, w * HD:(w + 1) * HD], x0], axis=0)
         carry[:, w * HD:(w + 1) * HD] = x0[ROWS - 8:]
-        y = taps_ref[3:4, w * HD:(w + 1) * HD] * x0
+        taps = tap_ref[:, c * HD:(c + 1) * HD].astype(f32)
+        y = taps[3:4] * x0
         for lag in (1, 2, 3):
-            t = taps_ref[3 - lag:4 - lag, w * HD:(w + 1) * HD]
+            t = taps[3 - lag:4 - lag]
             y = y + jnp.where(keep[lag], t * x[8 - lag:8 - lag + ROWS], 0.0)
         return y * sigmoid(y)
 
     def unit(x):
         return x * lax.rsqrt(jnp.sum(x * x, axis=-1, keepdims=True) + 1e-06)
 
-    qs = [unit(conv(q_ref, c, c)) * HD ** (-0.5) for c in range(2)]
-    ks = [unit(conv(k_ref, c, 2 + c)) for c in range(2)]
-    vs = [conv(v_ref, c, 4 + c) for c in range(4)]
+    qs = [unit(conv(q_ref, tq_ref, c, c)) * HD ** (-0.5) for c in range(2)]
+    ks = [unit(conv(k_ref, tk_ref, c, 2 + c)) for c in range(2)]
+    vs = [conv(v_ref, tv_ref, c, 4 + c) for c in range(4)]
     qb = [x.astype(bf16) for x in qs]
     kb = [x.astype(bf16) for x in ks]
     ba = ba_ref[...]
     beta = sigmoid(ba)
-    z = ba + dec_ref[0:1, :]
-    g = dec_ref[1:2, :] * (jnp.maximum(z, 0.0) + jnp.log1p(jnp.exp(-jnp.abs(z))))
+    lane = lax.broadcasted_iota(jnp.int32, (1, 8), 1)
+    bias, rate = jnp.zeros((1, 8), f32), jnp.zeros((1, 8), f32)
+    for h in range(4):
+        bias = jnp.where(lane == 4 + h, dt[h], bias)
+        rate = jnp.where(lane == 4 + h, -decay[h], rate)
+    z = ba + bias
+    g = rate * (jnp.maximum(z, 0.0) + jnp.log1p(jnp.exp(-jnp.abs(z))))
 
     ii = lax.broadcasted_iota(jnp.int32, (BLOCK, 256), 0)
     ll = lax.broadcasted_iota(jnp.int32, (BLOCK, 256), 1)
@@ -166,52 +172,208 @@
     for h in range(4):
         st_ref[h] = state[h]
 
-def local_scan(info, q, k, v, halo, ba, dec, taps):
-    n = q.shape[0]
-    row = lambda w: pl.BlockSpec((ROWS, w), lambda i: (i, 0))
+def local_scan(lens, dt, decay, raw, halo, ba, tq, tk, tv):
+    n = raw.shape[0]
+    row = lambda w, j=0: pl.BlockSpec((ROWS, w), lambda i: (i, j))
     whole = lambda s: pl.BlockSpec(s, lambda i: (0,) * len(s))
+    sm = pl.BlockSpec(memory_space=pltpu.SMEM)
     return pl.pallas_call(
         local_kernel,
         grid=(n // ROWS,),
-        in_specs=[pl.BlockSpec(memory_space=pltpu.SMEM), row(256), row(256), row(512),
-                  whole((8, 1024)), row(8), whole((2, 8)), whole((4, 1024))],
+        in_specs=[sm, sm, sm, row(256), row(256, 1), row(512, 1), whole((16, 1024)), row(8),
+                  whole((4, 256)), whole((4, 256)), whole((4, 512))],
         out_specs=[row(512), row(512), whole((4, HD, 2 * HD))],
         out_shape=[jax.ShapeDtypeStruct((n, 512), f32), jax.ShapeDtypeStruct((n, 512), bf16),
                    jax.ShapeDtypeStruct((4, HD, 2 * HD), f32)],
         scratch_shapes=[pltpu.VMEM((8, 1024), f32)],
         name="local_scan",
-    )(info, q, k, v, halo, ba, dec, taps)
+    )(lens, dt, decay, raw, raw, raw, halo, ba, tq, tk, tv)
 from jax.sharding import PartitionSpec as P
 
 MESH = pl.DeviceIdType.MESH
 TURNS = 8
 SEQ = 16
-
-
-def chain_kernel(t_ref, b_ref, in_ref, sent, held, send_sem, recv_sem):
+CHIPS = 4
+CHUNKS = 4
+DEEP = 2048
+
+
+class Later:
+    def __init__(self, make):
+        self.make = make
+
+    def start(self):
+        self.make().start()
+
+    def wait(self):
+        self.make().wait()
+
+    def wait_recv(self):
+        self.make().wait_recv()
+
+    def wait_send(self):
+        self.make().wait_send()
+
+
+def ring_places():
+    h = lax.axis_index("head")
+    z, c = h // 2, lax.rem(h, 2)
+    up = lax.rem(z + 1, CHIPS) * 2 + c
+    down = lax.rem(z + CHIPS - 1, CHIPS) * 2 + c
+    far = lax.rem(z + 2, CHIPS) * 2 + c
+    return h, z, c, up, down, far, z * 2 + 1 - c
+
+
+def greet(peers):
+    barrier = pltpu.get_barrier_semaphore()
+    for p in peers:
+        pl.semaphore_signal(barrier, inc=1, device_id=p, device_id_type=MESH)
+    pl.semaphore_wait(barrier, len(peers))
+
+
+def project_kernel(x_ref, wq, wk, wv, wz, wb, wa, raw_hbm, ba_ref, halo_ref,
+                   xg, w_all, wb_v, wa_v, raw_v, tail, landed, load_sem, store_sem, send_sem, recv_sem,
+                   tail_sem):
+    h, z, c, up, down, far, mate = ring_places()
     s = lax.axis_index("seq")
-    after = lax.rem(s + 1, SEQ)
-    barrier = pltpu.get_barrier_semaphore()
-    pl.semaphore_signal(
-        barrier, inc=1, device_id={"seq": lax.rem(s + SEQ - 1, SEQ)}, device_id_type=MESH)
-    pl.semaphore_wait(barrier, 1)
-
+    n = x_ref.shape[0]
+    rc = n // CHUNKS
+    half = rc // 2
+    loads = [pltpu.make_async_copy(a, b, load_sem.at[i]) for i, (a, b) in enumerate((
+        (wq, w_all.at[:, 0:256]), (wk, w_all.at[:, 256:512]), (wv, w_all.at[:, 512:1024]),
+        (wz, w_all.at[:, 1024:1536]), (wb, wb_v), (wa, wa_v)))]
+    for cp in loads:
+        cp.start()
+    own = pl.ds(pl.multiple_of(h * 256, 256), 256)
+    after = {"seq": lax.rem(s + 1, SEQ)}
+    before = {"seq": lax.rem(s + SEQ - 1, SEQ)}
+    greet([{"head": up}, {"head": down}, {"head": mate}, after, before])
+
+    def cols(b):
+        return pl.ds(pl.multiple_of(b * 256, 256), 256)
+
+    def move(r, kind, src, rows, block, to):
+        return Later(lambda: pltpu.make_async_remote_copy(
+            src_ref=src, dst_ref=xg.at[rows, cols(block)], send_sem=send_sem.at[r, kind],
+            recv_sem=recv_sem.at[r, kind], device_id={"head": to}, device_id_type=MESH))
+
+    def rows_of(r):
+        return pl.ds(r * rc, rc)
+
+    def near(r):
+        rows = rows_of(r)
+        return [move(r, 0, x_ref.at[rows, :], rows, h, up), move(r, 1, x_ref.at[rows, :], rows, h, down),
+                move(r, 2, x_ref.at[rows, :], rows, h, mate)]
+
+    def relay(r):
+        rows, ra, rb = rows_of(r), pl.ds(r * rc, half), pl.ds(r * rc + half, half)
+        return [move(r, 3, xg.at[ra, cols(down)], ra, down, up),
+                move(r, 4, xg.at[rb, cols(up)], rb, up, down),
+                move(r, 5, xg.at[rows, cols(down)], rows, down, mate),
+                move(r, 6, xg.at[rows, cols(up)], rows, up, mate)]
+
+    def across(r):
+        ra, rb = pl.ds(r * rc, half), pl.ds(r * rc + half, half)
+        return [move(r, 7, xg.at[ra, cols(far)], ra, far, mate),
+                move(r, 8, xg.at[rb, cols(far)], rb, far, mate)]
+
+    order = [CHUNKS - 1] + list(range(CHUNKS - 1))
+    for r in order:
+        for cp in near(r):
+            cp.start()
+    xg[:, own] = x_ref[...]
+    give = pltpu.make_async_remote_copy(
+        src_ref=tail, dst_ref=landed, send_sem=tail_sem.at[0], recv_sem=tail_sem.at[1],
+        device_id=after, device_id_type=MESH)
+
+    def relay_stage(r):
+        a, b, _ = near(r)
+        fa, fb, ma, mb = relay(r)
+        a.wait_recv()
+        fa.start()
+        ma.start()
+        b.wait_recv()
+        fb.start()
+        mb.start()
+
+    def across_stage(r):
+        fa, fb, _, _ = relay(r)
+        ca, cb = across(r)
+        fa.wait_recv()
+        ca.start()
+        fb.wait_recv()
+        cb.start()
+
+    def multiply(i, r):
+        near(r)[2].wait_recv()
+        for cp in relay(r)[2:] + across(r):
+            cp.wait_recv()
+        if i == 0:
+            for cp in loads:
+                cp.wait()
+        x = xg[r * rc:(r + 1) * rc, :]
+        rs = slice(r * rc, (r + 1) * rc)
+        ba_ref[rs, 0:4] = dotf(x, wb_v[...])
+        ba_ref[rs, 4:8] = dotf(x, wa_v[...])
+        for j in range(6):
+            raw_v[rs, j * 256:(j + 1) * 256] = dotf(x, w_all[:, j * 256:(j + 1) * 256]).astype(bf16)
+        if i == 0:
+            tail[...] = raw_v[n - 16:, 0:1024]
+            give.start()
+        pltpu.make_async_copy(raw_v.at[rs, :], raw_hbm.at[rs, :], store_sem.at[r]).start()
+
+    for i in range(CHUNKS + 2):
+        if i < CHUNKS:
+            relay_stage(order[i])
+        if 1 <= i < CHUNKS + 1:
+            across_stage(order[i - 1])
+        if i >= 2:
+            multiply(i - 2, order[i - 2])
+    give.wait()
+    halo_ref[...] = landed[...]
+    for r in order:
+        for cp in near(r) + relay(r) + across(r):
+            cp.wait_send()
+        rs = slice(r * rc, (r + 1) * rc)
+        pltpu.make_async_copy(raw_v.at[rs, :], raw_hbm.at[rs, :], store_sem.at[r]).wait()
+
+
+def project(x, wq, wk, wv, wz, wb, wa):
+    n = x.shape[0]
+    vm, anyw = pl.BlockSpec(memory_space=pltpu.VMEM), pl.BlockSpec(memory_space=pl.ANY)
+    return pl.pallas_call(
+        project_kernel,
+        in_specs=[vm] + [anyw] * 6, out_specs=[anyw, vm, vm],
+        out_shape=[jax.ShapeDtypeStruct((n, 1536), bf16), jax.ShapeDtypeStruct((n, 8), f32),
+                   jax.ShapeDtypeStruct((16, 1024), bf16)],
+        scratch_shapes=[
+            pltpu.VMEM((n, DEEP), bf16), pltpu.VMEM((DEEP, 1536), bf16), pltpu.VMEM((DEEP, 4), bf16),
+            pltpu.VMEM((DEEP, 4), bf16), pltpu.VMEM((n, 1536), bf16), pltpu.VMEM((16, 1024), bf16),
+            pltpu.VMEM((16, 1024), bf16), pltpu.SemaphoreType.DMA((6,)), pltpu.SemaphoreType.DMA((CHUNKS,)),
+            pltpu.SemaphoreType.DMA((CHUNKS, 9)), pltpu.SemaphoreType.DMA((CHUNKS, 9)),
+            pltpu.SemaphoreType.DMA((2,))],
+        compiler_params=pltpu.CompilerParams(collective_id=2, has_side_effects=True),
+        name="project",
+    )(x, wq, wk, wv, wz, wb, wa)
+
+
+def chain(t_of, b_of, sent, held, send_sem, recv_sem, after):
     def hop(t, h):
         return pltpu.make_async_remote_copy(
             src_ref=sent.at[t, h], dst_ref=held.at[t, h], send_sem=send_sem.at[t, h],
-            recv_sem=recv_sem.at[t, h], device_id={"seq": after}, device_id_type=MESH)
+            recv_sem=recv_sem.at[t, h], device_id=after, device_id_type=MESH)
 
     for h in range(4):
-        sent[0, h] = b_ref[h].astype(bf16)
+        sent[0, h] = b_of(h).astype(bf16)
         hop(0, h).start()
 
     def turn(t, carry):
         for h in range(4):
             hop(t - 1, h).wait_recv()
             arrived = held[t - 1, h]
-            hi, lo = split2(t_ref[h])
+            hi, lo = split2(t_of(h))
             out = dotf(jnp.concatenate([hi, lo], axis=1),
-                       jnp.concatenate([arrived, arrived], axis=0)) + b_ref[h]
+                       jnp.concatenate([arrived, arrived], axis=0)) + b_of(h)
             sent[t, h] = out.astype(bf16)
             hop(t, h).start()
         return carry
@@ -219,72 +381,153 @@
     lax.fori_loop(1, TURNS, turn, 0)
     for h in range(4):
         hop(TURNS - 1, h).wait_recv()
-        in_ref[h] = held[TURNS - 1, h]
 
     def drain(t, carry):
         for h in range(4):
             hop(t, h).wait_send()
         return carry
 
-    lax.fori_loop(0, TURNS, drain, 0)
-
-
-def hand_over(across, local_state):
-    vm = pl.BlockSpec(memory_space=pltpu.VMEM)
+    return [held[TURNS - 1, h] for h in range(4)], lambda: lax.fori_loop(0, TURNS, drain, 0)
+
+
+def output_kernel(st_ref, o_hbm, l_hbm, raw_hbm, nw_ref, w_hbm, out_ref,
+                  o_v, l_v, z_v, w_v, sent, held, mine, theirs, given, pass_out, pass_in, to_up, to_down,
+                  from_down, from_up, load_sem, c_send, c_recv, p_send, p_recv, send_sem, recv_sem):
+    h, z, c, up, down, far, mate = ring_places()
+    s = lax.axis_index("seq")
+    n = o_v.shape[0]
+    rc = n // CHUNKS
+    half = rc // 2
+    loads = [pltpu.make_async_copy(a, b, load_sem.at[i]) for i, (a, b) in enumerate((
+        (o_hbm, o_v), (l_hbm, l_v), (raw_hbm.at[:, 1024:1536], z_v), (w_hbm, w_v)))]
+    for cp in loads:
+        cp.start()
+    after = {"seq": lax.rem(s + 1, SEQ)}
+    before = {"seq": lax.rem(s + SEQ - 1, SEQ)}
+    greet([{"head": up}, {"head": down}, {"head": mate}, after, before])
+    s_in, drained = chain(lambda i: st_ref[i, :, HD:], lambda i: st_ref[i, :, :HD],
+                          sent, held, c_send, c_recv, after)
+    for cp in loads:
+        cp.wait()
+
+    def remote(src, dst, ss, rs, to):
+        return Later(lambda: pltpu.make_async_remote_copy(
+            src_ref=src, dst_ref=dst, send_sem=ss, recv_sem=rs, device_id={"head": to},
+            device_id_type=MESH))
+
+    def swap(r, j):
+        return remote(given.at[r, j], theirs.at[r, j], p_send.at[r, j], p_recv.at[r, j], mate)
+
+    def copies(r):
+        a, b = pl.ds(0, half), pl.ds(half, half)
+        sem = lambda k: (send_sem.at[r, k], recv_sem.at[r, k])
+        return [remote(pass_out.at[r, a], pass_in.at[r, a], *sem(0), up),
+                remote(pass_out.at[r, b], pass_in.at[r, b], *sem(1), down),
+                remote(to_up.at[r, b], from_down.at[r, b], *sem(2), up),
+                remote(to_down.at[r, a], from_up.at[r, a], *sem(3), down),
+                remote(to_up.at[r, a], from_down.at[r, a], *sem(4), up),
+                remote(to_down.at[r, b], from_up.at[r, b], *sem(5), down)]
+
+    def wcols(b):
+        return pl.ds(pl.multiple_of(b * 256, 256), 256)
+
+    def chip(j):
+        return lax.rem(z + j, CHIPS)
+
+    def share(r):
+        rs = slice(r * rc, (r + 1) * rc)
+        parts = []
+        for i in range(4):
+            hc = slice(i * HD, (i + 1) * HD)
+            o = o_v[rs, hc] + dotf(l_v[rs, hc], s_in[i])
+            var = jnp.mean(o * o, axis=-1, keepdims=True)
+            g = z_v[rs, hc].astype(f32)
+            parts.append((o * lax.rsqrt(var + 1e-06) * nw_ref[...] * (g * sigmoid(g))).astype(bf16))
+        normed = jnp.concatenate(parts, axis=1)
+        for j in (2, 1, 3, 0):
+            given[r, j] = dotf(normed, w_v[:, wcols(chip(j) * 2 + 1 - c)]).astype(bf16)
+            swap(r, j).start()
+        for j in (2, 1, 3, 0):
+            mine[r, j] = dotf(normed, w_v[:, wcols(chip(j) * 2 + c)])
+
+    def both(r, j):
+        return mine[r, j] + theirs[r, j].astype(f32)
+
+    def leave(r):
+        cps = copies(r)
+        swap(r, 2).wait_recv()
+        pass_out[r] = both(r, 2).astype(bf16)
+        cps[0].start()
+        cps[1].start()
+        swap(r, 1).wait_recv()
+        to_up[r, half:] = both(r, 1)[half:].astype(bf16)
+        cps[2].start()
+        swap(r, 3).wait_recv()
+        to_down[r, :half] = both(r, 3)[:half].astype(bf16)
+        cps[3].start()
+
+    def add_on(r):
+        cps = copies(r)
+        cps[0].wait_recv()
+        to_up[r, :half] = (both(r, 1)[:half] + pass_in[r, :half].astype(f32)).astype(bf16)
+        cps[4].start()
+        cps[1].wait_recv()
+        to_down[r, half:] = (both(r, 3)[half:] + pass_in[r, half:].astype(f32)).astype(bf16)
+        cps[5].start()
+
+    def finish(r):
+        for cp in copies(r)[2:]:
+            cp.wait_recv()
+        swap(r, 0).wait_recv()
+        out_ref[r * rc:(r + 1) * rc, :] = (
+            both(r, 0) + from_down[r].astype(f32) + from_up[r].astype(f32)).astype(bf16)
+
+    for i in range(CHUNKS + 3):
+        if i < CHUNKS:
+            share(i)
+        if 1 <= i < CHUNKS + 1:
+            leave(i - 1)
+        if 2 <= i < CHUNKS + 2:
+            add_on(i - 2)
+        if i >= 3:
+            finish(i - 3)
+    drained()
+    for r in range(CHUNKS):
+        for j in range(4):
+            swap(r, j).wait_send()
+        for cp in copies(r):
+            cp.wait_send()
+
+
+def output(st, o, lift, raw, nw, w):
+    n = o.shape[0]
+    rc = n // CHUNKS
+    vm, anyw = pl.BlockSpec(memory_space=pltpu.VMEM), pl.BlockSpec(memory_space=pl.ANY)
+    buf = pltpu.VMEM((CHUNKS, rc, 256), bf16)
+    dma = pltpu.SemaphoreType.DMA
     return pl.pallas_call(
-        chain_kernel,
-        in_specs=[vm, vm], out_specs=vm,
-        out_shape=jax.ShapeDtypeStruct((4, HD, HD), bf16),
-        scratch_shapes=[pltpu.VMEM((TURNS, 4, HD, HD), bf16), pltpu.VMEM((TURNS, 4, HD, HD), bf16),
-                        pltpu.SemaphoreType.DMA((TURNS, 4)), pltpu.SemaphoreType.DMA((TURNS, 4))],
-        compiler_params=pltpu.CompilerParams(collective_id=1, has_side_effects=True),
-        name="hand_over",
-    )(across, local_state)
-
-
-def gated_rows(o_ref, l_ref, s_ref, z_ref, nw_ref, r):
-    cols = []
-    for h in range(4):
-        c = slice(h * HD, (h + 1) * HD)
-        o = o_ref[r, c] + dotf(l_ref[r, c], s_ref[h])
-        var = jnp.mean(o * o, axis=-1, keepdims=True)
-        z = z_ref[r, c].astype(f32)
-        cols.append((o * lax.rsqrt(var + 1e-06) * nw_ref[...] * (z * sigmoid(z))).astype(bf16))
-    return jnp.concatenate(cols, axis=1)
-
-
-def out_kernel(o_ref, l_ref, s_ref, z_ref, nw_ref, w_ref, p_ref):
-    normed = gated_rows(o_ref, l_ref, s_ref, z_ref, nw_ref, slice(None))
-    p_ref[...] = dotf(normed, w_ref[...]).astype(bf16)
-
-
-def out_share(o, lift, s_in, z, nw, w):
-    n = o.shape[0]
-    row = lambda w: pl.BlockSpec((ROWS, w), lambda i: (i, 0))
-    whole = lambda s: pl.BlockSpec(s, lambda i: (0,) * len(s))
-    return pl.pallas_call(
-        out_kernel, grid=(n // ROWS,),
-        in_specs=[row(512), row(512), whole((4, HD, HD)), row(512), whole((1, HD)), whole((512, 2048))],
-        out_specs=row(2048), out_shape=jax.ShapeDtypeStruct((n, 2048), bf16), name="out_share",
-    )(o, lift, s_in, z, nw, w)
+        output_kernel,
+        in_specs=[vm, anyw, anyw, anyw, vm, anyw], out_specs=vm,
+        out_shape=jax.ShapeDtypeStruct((n, 256), bf16),
+        scratch_shapes=[
+            pltpu.VMEM((n, 512), f32), pltpu.VMEM((n, 512), bf16), pltpu.VMEM((n, 512), bf16),
+            pltpu.VMEM((512, 2048), bf16), pltpu.VMEM((TURNS, 4, HD, HD), bf16),
+            pltpu.VMEM((TURNS, 4, HD, HD), bf16), pltpu.VMEM((CHUNKS, 4, rc, 256), f32),
+            pltpu.VMEM((CHUNKS, 4, rc, 256), bf16), pltpu.VMEM((CHUNKS, 4, rc, 256), bf16),
+            buf, buf, buf, buf, buf, buf,
+            dma((4,)), dma((TURNS, 4)), dma((TURNS, 4)), dma((CHUNKS, 4)), dma((CHUNKS, 4)),
+            dma((CHUNKS, 6)), dma((CHUNKS, 6))],
+        compiler_params=pltpu.CompilerParams(collective_id=3, has_side_effects=True),
+        name="output",
+    )(st, o, lift, raw, nw, w)
 
 
 def per_device(hidden_in, w_query, w_key, w_value, w_gate, w_beta, w_alpha, dt_bias, head_decay,
                conv_query, conv_key, conv_value, norm_weight, w_out, prompt_lengths):
-    n = hidden_in.shape[0]
-    columns_in = lax.all_gather(hidden_in, "head", axis=1, tiled=True)
-    q, k, v, z = (dotf(columns_in, w).astype(bf16) for w in (w_query, w_key, w_value, w_gate))
-    ba = dotf(columns_in, jnp.concatenate([w_beta, w_alpha], axis=1))
-    tails = jnp.concatenate([q[n - 8:], k[n - 8:], v[n - 8:]], axis=1)
-    halo = lax.ppermute(tails, "seq", [(i, i + 1) for i in range(SEQ - 1)]).astype(f32)
-    info = jnp.concatenate([jnp.reshape(lax.axis_index("seq") * n, (1,)), prompt_lengths]).astype(jnp.int32)
-    zero4 = jnp.zeros((4,), f32)
-    dec = jnp.stack([jnp.concatenate([zero4, dt_bias]), jnp.concatenate([zero4, -head_decay])])
-    taps = jnp.concatenate([conv_query, conv_key, conv_value], axis=1).astype(f32)
-    o, lift, st = local_scan(info, q, k, v, halo, ba, dec, taps)
-    s_in = hand_over(st[:, :, HD:], st[:, :, :HD])
-    part = out_share(o, lift, s_in, z, norm_weight[None, :], w_out)
-    return lax.psum_scatter(part, "head", scatter_dimension=1, tiled=True)
+    raw, ba, halo = project(hidden_in, w_query, w_key, w_value, w_gate, w_beta, w_alpha)
+    o, lift, st = local_scan(prompt_lengths, dt_bias, head_decay, raw, halo, ba,
+                             conv_query, conv_key, conv_value)
+    return output(st, o, lift, raw, norm_weight[None, :], w_out)
 
 
 def solution(mesh):

time: 176 us -> 124 us (0.70)
  waiting for transfers between devices: 73.4 us -> 0 us
  Pallas kernels: 64.4 us -> 117 us
  between operations: 13.5 us -> 0.02 us
  matrix products: 12.8 us -> 0 us
  other arithmetic: 4.34 us -> 0 us
  starting transfers between devices: 3.74 us -> 0 us
  local copies, waits for them, and re-layouts: 3.44 us -> 5.41 us
    pallas_call x3, Pallas kernels: 64.4 us -> 117 us  [the longest x1 58.1 us: output(): pl.pallas_call(output_kernel, in_specs=[vm, anyw, anyw, anyw, vm, anyw],...]
    reduce_scatter x1 -> x0, waiting for transfers between devices: 37.2 us -> none  [per_device(): return lax.psum_scatter(part, 'head', scatter_dimension=1, tiled=True)]
    all_gather x1 -> x0, waiting for transfers between devices: 35.5 us -> none  [per_device(): columns_in = lax.all_gather(hidden_in, 'head', axis=1, tiled=True)]
    dot_general x5 -> x0, matrix products: 12.8 us -> none  [dotf(): return jnp.dot(a, b, preferred_element_type=f32)]
    unnamed x18 -> x3, local copies, waits for them, and re-layouts: 0.82 us -> 5.41 us
    ppermute x1 -> x0, starting transfers between devices: 3.7 us -> none  [per_device(): lax.ppermute(tails, 'seq', [(i, i + 1) for i in range(SEQ - 1)]).astype(f32)]
    convert_element_type x2 -> x0, other arithmetic: 1.92 us -> none  [the longest x1 1.31 us: per_device(): jnp.concatenate([conv_query, conv_key, conv_value], axis=1).astype(f32)]
    slice x4 -> x0, local copies, waits for them, and re-layouts: 1.89 us -> none  [the longest x1 1.88 us: per_device(): s_in = hand_over(st[:, :, HD:], st[:, :, :HD])]
  transfers between devices with their start and end apart: 3 -> 0, of which waited for: 2 -> 0; matrix products, arithmetic and copies ran while one was open for 6% -> 0% of each run, Pallas kernels for 0% -> 0%
where the time goes in v2:
time: 124 us; the launch traced here: 123 us
  Pallas kernels  117 us (94%)
  local copies, waits for them, and re-layouts  5.41 us (4%)
    pallas_call x1, Pallas kernels, output(): pl.pallas_call(output_kernel, in_specs=[vm, anyw, anyw, anyw, vm, anyw],...  58.1 us
    pallas_call x1, Pallas kernels, project(): pl.pallas_call(project_kernel, in_specs=[vm] + [anyw] * 6, out_specs=[any...  37.6 us
    pallas_call x1, Pallas kernels, local_scan(): pl.pallas_call(local_kernel, grid=(n // ROWS,), in_specs=[sm, sm, sm, row...  21.8 us
    unnamed x3, local copies, waits for them, and re-layouts  5.41 us

profile of v2, /device:TPU:0, one launch (start us, length us, event | category | flops | bytes accessed | tf_op | source)
XLA Modules:
  0.0 122.8 jit_solution(11320048410439806790)
XLA Ops:
  0.0 1.8 %copy.16.wb = bf16[2048,4]{1,0:T(8,128)(2,1)} copy(bf16[2048,4]{0,1:T(4,128)(2,1)} %param.20) | data formatting | bytes 32768 | tf_op args[5]
  1.8 1.8 %copy.17.wa = bf16[2048,4]{1,0:T(8,128)(2,1)} copy(bf16[2048,4]{0,1:T(4,128)(2,1)} %param.21) | data formatting | bytes 32768 | tf_op args[6]
  3.5 37.6 %project.1 = (bf16[1024,1536]{1,0:T(8,128)(2,1)}, f32[1024,8]{1,0:T(8,128)}, bf16[16,1024]{1,0:T(8,128)(2,1)}) custom-call(bf16[1024,256]{1,0:T(8,128)(2,1)} %x_ref.1, bf16[2048,256]{1,0:T(8,128)(2,1)} %wq.1, bf16[2048,256]{1,0:T(8,128)(2,1)} %wk.1, bf16[2048,512]{1,0:T(8,128)(2,1)} %wv.1, bf16[2048,512]{1,0:T(8,128)(2,1)} %wz.1, bf16[2048,4]{1,0:T(8,128)(2,1)} %copy.16.wb, ...), custom_call_target="tpu_custom_call" | custom-call | tf_op jit(solution)/shard_map/project/pallas_call | solution.py:344
  41.1 21.8 %local_scan.1 = (f32[1024,512]{1,0:T(8,128)}, bf16[1024,512]{1,0:T(8,128)(2,1)}, f32[4,128,256]{2,1,0:T(8,128)}) custom-call(s32[6]{0:T(128)} %lens.1, f32[4]{0:T(128)} %dt.1, f32[4]{0:T(128)} %decay.1, bf16[1024,1536]{1,0:T(8,128)(2,1)} %get-tuple-element.11.q_ref.k_ref.v_ref.raw_hbm, bf16[1024,1536]{1,0:T(8,128)(2,1)} %get-tuple-element.11.q_ref.k_ref.v_ref.raw_hbm, ...), custom_call_target="tpu_custom_call" | custom-call | tf_op jit(solution)/shard_map/local_scan/pallas_call | solution.py:180
  62.9 58.1 %output.1 = bf16[1024,256]{1,0:T(8,128)(2,1)} custom-call(f32[4,128,256]{2,1,0:T(8,128)} %get-tuple-element.14.st_ref, f32[1024,512]{1,0:T(8,128)} %get-tuple-element.15.o_hbm, bf16[1024,512]{1,0:T(8,128)(2,1)} %get-tuple-element.16.l_hbm, bf16[1024,1536]{1,0:T(8,128)(2,1)} %get-tuple-element.11.q_ref.k_ref.v_ref.raw_hbm, f32[1,128]{1,0:T(1,128)} %bitcast.1, ...), custom_call_target="tpu_custom_call" | custom-call | tf_op jit(solution)/shard_map/output/pallas_call | solution.py:508
  121.0 1.9 %copy.19 = bf16[1024,256]{1,0:T(8,128)(2,1)} copy(bf16[1024,256]{1,0:T(8,128)(2,1)} %output.1) | data formatting | bytes 1048576

commit v3 on v2

--- a/solution.py
+++ b/solution.py
@@ -21,20 +21,8 @@
 def sigmoid(x):
     return 1.0 / (1.0 + jnp.exp(-x))
 
-def local_kernel(lens, dt, decay, q_ref, k_ref, v_ref, halo_ref, ba_ref, tq_ref, tk_ref, tv_ref,
-                 out_ref, lift_ref, st_ref, carry):
-    step = pl.program_id(0)
-
-    @pl.when(step == 0)
-    def _():
-        rows = lax.broadcasted_iota(jnp.int32, (HD, 2 * HD), 0)
-        cols = lax.broadcasted_iota(jnp.int32, (HD, 2 * HD), 1)
-        init = jnp.where(cols - HD == rows, 1.0, 0.0).astype(f32)
-        for h in range(4):
-            st_ref[h] = init
-        carry[...] = halo_ref[8:].astype(f32)
-
-    base = (lax.axis_index("seq") * pl.num_programs(0) + step) * ROWS
+def scan_rows(base, lens, dt, decay, q_ref, k_ref, v_ref, ba_ref, tq_ref, tk_ref, tv_ref,
+              out_ref, lift_ref, st_ref, carry):
     pos = base + lax.broadcasted_iota(jnp.int32, (ROWS, HD), 0)
     start = jnp.zeros((ROWS, HD), jnp.int32)
     off = lens[0] * 0
@@ -172,26 +160,12 @@
     for h in range(4):
         st_ref[h] = state[h]
 
-def local_scan(lens, dt, decay, raw, halo, ba, tq, tk, tv):
-    n = raw.shape[0]
-    row = lambda w, j=0: pl.BlockSpec((ROWS, w), lambda i: (i, j))
-    whole = lambda s: pl.BlockSpec(s, lambda i: (0,) * len(s))
-    sm = pl.BlockSpec(memory_space=pltpu.SMEM)
-    return pl.pallas_call(
-        local_kernel,
-        grid=(n // ROWS,),
-        in_specs=[sm, sm, sm, row(256), row(256, 1), row(512, 1), whole((16, 1024)), row(8),
-                  whole((4, 256)), whole((4, 256)), whole((4, 512))],
-        out_specs=[row(512), row(512), whole((4, HD, 2 * HD))],
-        out_shape=[jax.ShapeDtypeStruct((n, 512), f32), jax.ShapeDtypeStruct((n, 512), bf16),
-                   jax.ShapeDtypeStruct((4, HD, 2 * HD), f32)],
-        scratch_shapes=[pltpu.VMEM((8, 1024), f32)],
-        name="local_scan",
-    )(lens, dt, decay, raw, raw, raw, halo, ba, tq, tk, tv)
+
 from jax.sharding import PartitionSpec as P
 
 MESH = pl.DeviceIdType.MESH
-TURNS = 8
+SIDE = 4
+OUT_CHUNKS = 8
 SEQ = 16
 CHIPS = 4
 CHUNKS = 4
@@ -231,9 +205,10 @@
     pl.semaphore_wait(barrier, len(peers))
 
 
-def project_kernel(x_ref, wq, wk, wv, wz, wb, wa, raw_hbm, ba_ref, halo_ref,
-                   xg, w_all, wb_v, wa_v, raw_v, tail, landed, load_sem, store_sem, send_sem, recv_sem,
-                   tail_sem):
+def project_kernel(lens, dt, decay, x_ref, wq, wk, wv, wz, wb, wa, tq_ref, tk_ref, tv_ref,
+                   o_hbm, l_hbm, z_hbm, st_ref,
+                   xg, w_all, wb_v, wa_v, wba, raw_v, ba_v, o_v, l_v, carry, tail, landed,
+                   load_sem, store_sem, send_sem, recv_sem, tail_sem):
     h, z, c, up, down, far, mate = ring_places()
     s = lax.axis_index("seq")
     n = x_ref.shape[0]
@@ -257,8 +232,11 @@
             src_ref=src, dst_ref=xg.at[rows, cols(block)], send_sem=send_sem.at[r, kind],
             recv_sem=recv_sem.at[r, kind], device_id={"head": to}, device_id_type=MESH))
 
+    def span(first, size):
+        return pl.ds(pl.multiple_of(first, size), size)
+
     def rows_of(r):
-        return pl.ds(r * rc, rc)
+        return span(r * rc, rc)
 
     def near(r):
         rows = rows_of(r)
@@ -266,25 +244,31 @@
                 move(r, 2, x_ref.at[rows, :], rows, h, mate)]
 
     def relay(r):
-        rows, ra, rb = rows_of(r), pl.ds(r * rc, half), pl.ds(r * rc + half, half)
+        rows, ra, rb = rows_of(r), span(r * rc, half), span(r * rc + half, half)
         return [move(r, 3, xg.at[ra, cols(down)], ra, down, up),
                 move(r, 4, xg.at[rb, cols(up)], rb, up, down),
                 move(r, 5, xg.at[rows, cols(down)], rows, down, mate),
                 move(r, 6, xg.at[rows, cols(up)], rows, up, mate)]
 
     def across(r):
-        ra, rb = pl.ds(r * rc, half), pl.ds(r * rc + half, half)
+        ra, rb = span(r * rc, half), span(r * rc + half, half)
         return [move(r, 7, xg.at[ra, cols(far)], ra, far, mate),
                 move(r, 8, xg.at[rb, cols(far)], rb, far, mate)]
 
-    order = [CHUNKS - 1] + list(range(CHUNKS - 1))
-    for r in order:
-        for cp in near(r):
+    def place(i):
+        return lax.rem(i + CHUNKS - 1, CHUNKS)
+
+    for i in (0, 1):
+        for cp in near(place(i)):
             cp.start()
     xg[:, own] = x_ref[...]
-    give = pltpu.make_async_remote_copy(
+    rows_i = lax.broadcasted_iota(jnp.int32, (HD, 2 * HD), 0)
+    cols_i = lax.broadcasted_iota(jnp.int32, (HD, 2 * HD), 1)
+    for i in range(4):
+        st_ref[i] = jnp.where(cols_i - HD == rows_i, 1.0, 0.0).astype(f32)
+    give = Later(lambda: pltpu.make_async_remote_copy(
         src_ref=tail, dst_ref=landed, send_sem=tail_sem.at[0], recv_sem=tail_sem.at[1],
-        device_id=after, device_id_type=MESH)
+        device_id=after, device_id_type=MESH))
 
     def relay_stage(r):
         a, b, _ = near(r)
@@ -304,109 +288,171 @@
         fb.wait_recv()
         cb.start()
 
-    def multiply(i, r):
+    def stores(r):
+        rows = rows_of(r)
+        return [Later(lambda a=a, b=b, j=j: pltpu.make_async_copy(a, b, store_sem.at[r, j]))
+                for j, (a, b) in enumerate((
+                    (o_v.at[rows, :], o_hbm.at[rows, :]), (l_v.at[rows, :], l_hbm.at[rows, :]),
+                    (raw_v.at[rows, 1024:1536], z_hbm.at[rows, :])))]
+
+    def multiply(r):
         near(r)[2].wait_recv()
         for cp in relay(r)[2:] + across(r):
             cp.wait_recv()
-        if i == 0:
+        rs = rows_of(r)
+        x = xg[rs, :]
+        ba_v[rs, :] = lax.dot_general(x, wba[...], (((1,), (1,)), ((), ())), preferred_element_type=f32)
+        for j in range(6):
+            raw_v[rs, j * 256:(j + 1) * 256] = dotf(x, w_all[:, j * 256:(j + 1) * 256]).astype(bf16)
+
+    def scan(r):
+        rs = rows_of(r)
+        scan_rows((s * CHUNKS + r) * rc, lens, dt, decay, raw_v.at[rs, 0:256], raw_v.at[rs, 256:512],
+                  raw_v.at[rs, 512:1024], ba_v.at[rs, :], tq_ref, tk_ref, tv_ref,
+                  o_v.at[rs, :], l_v.at[rs, :], st_ref, carry)
+        for cp in stores(r):
+            cp.start()
+
+    def stage(i, none):
+        @pl.when(i < CHUNKS)
+        def _():
+            relay_stage(place(i))
+
+        @pl.when(i + 2 < CHUNKS)
+        def _():
+            for cp in near(place(i + 2)):
+                cp.start()
+
+        @pl.when((i >= 1) & (i < CHUNKS + 1))
+        def _():
+            across_stage(place(i + CHUNKS - 1))
+
+        @pl.when(i == 2)
+        def _():
             for cp in loads:
                 cp.wait()
-        x = xg[r * rc:(r + 1) * rc, :]
-        rs = slice(r * rc, (r + 1) * rc)
-        ba_ref[rs, 0:4] = dotf(x, wb_v[...])
-        ba_ref[rs, 4:8] = dotf(x, wa_v[...])
-        for j in range(6):
-            raw_v[rs, j * 256:(j + 1) * 256] = dotf(x, w_all[:, j * 256:(j + 1) * 256]).astype(bf16)
-        if i == 0:
+            wba[...] = jnp.concatenate(
+                [wb_v[...].astype(f32), wa_v[...].astype(f32)], axis=0).astype(bf16)
+
+        @pl.when((i >= 2) & (i < CHUNKS + 2))
+        def _():
+            multiply(place(i + CHUNKS - 2))
+
+        @pl.when(i == 2)
+        def _():
             tail[...] = raw_v[n - 16:, 0:1024]
             give.start()
-        pltpu.make_async_copy(raw_v.at[rs, :], raw_hbm.at[rs, :], store_sem.at[r]).start()
-
-    for i in range(CHUNKS + 2):
-        if i < CHUNKS:
-            relay_stage(order[i])
-        if 1 <= i < CHUNKS + 1:
-            across_stage(order[i - 1])
-        if i >= 2:
-            multiply(i - 2, order[i - 2])
-    give.wait()
-    halo_ref[...] = landed[...]
-    for r in order:
+
+        @pl.when(i == 3)
+        def _():
+            give.wait_recv()
+            carry[...] = landed[8:].astype(f32)
+
+        @pl.when(i >= 3)
+        def _():
+            scan(i - 3)
+        return none
+
+    lax.fori_loop(0, CHUNKS + 3, stage, 0)
+    give.wait_send()
+
+    def drain(r, none):
         for cp in near(r) + relay(r) + across(r):
             cp.wait_send()
-        rs = slice(r * rc, (r + 1) * rc)
-        pltpu.make_async_copy(raw_v.at[rs, :], raw_hbm.at[rs, :], store_sem.at[r]).wait()
-
-
-def project(x, wq, wk, wv, wz, wb, wa):
+        for cp in stores(r):
+            cp.wait()
+        return none
+
+    lax.fori_loop(0, CHUNKS, drain, 0)
+
+
+def project(lens, dt, decay, x, wq, wk, wv, wz, wb, wa, tq, tk, tv):
     n = x.shape[0]
     vm, anyw = pl.BlockSpec(memory_space=pltpu.VMEM), pl.BlockSpec(memory_space=pl.ANY)
+    sm = pl.BlockSpec(memory_space=pltpu.SMEM)
+    dma = pltpu.SemaphoreType.DMA
     return pl.pallas_call(
         project_kernel,
-        in_specs=[vm] + [anyw] * 6, out_specs=[anyw, vm, vm],
-        out_shape=[jax.ShapeDtypeStruct((n, 1536), bf16), jax.ShapeDtypeStruct((n, 8), f32),
-                   jax.ShapeDtypeStruct((16, 1024), bf16)],
+        in_specs=[sm, sm, sm, vm] + [anyw] * 6 + [vm] * 3, out_specs=[anyw, anyw, anyw, vm],
+        out_shape=[jax.ShapeDtypeStruct((n, 512), f32), jax.ShapeDtypeStruct((n, 512), bf16),
+                   jax.ShapeDtypeStruct((n, 512), bf16), jax.ShapeDtypeStruct((4, HD, 2 * HD), f32)],
         scratch_shapes=[
-            pltpu.VMEM((n, DEEP), bf16), pltpu.VMEM((DEEP, 1536), bf16), pltpu.VMEM((DEEP, 4), bf16),
-            pltpu.VMEM((DEEP, 4), bf16), pltpu.VMEM((n, 1536), bf16), pltpu.VMEM((16, 1024), bf16),
-            pltpu.VMEM((16, 1024), bf16), pltpu.SemaphoreType.DMA((6,)), pltpu.SemaphoreType.DMA((CHUNKS,)),
-            pltpu.SemaphoreType.DMA((CHUNKS, 9)), pltpu.SemaphoreType.DMA((CHUNKS, 9)),
-            pltpu.SemaphoreType.DMA((2,))],
+            pltpu.VMEM((n, DEEP), bf16), pltpu.VMEM((DEEP, 1536), bf16), pltpu.VMEM((4, DEEP), bf16),
+            pltpu.VMEM((4, DEEP), bf16), pltpu.VMEM((8, DEEP), bf16), pltpu.VMEM((n, 1536), bf16),
+            pltpu.VMEM((n, 8), f32), pltpu.VMEM((n, 512), f32), pltpu.VMEM((n, 512), bf16),
+            pltpu.VMEM((8, 1024), f32), pltpu.VMEM((16, 1024), bf16), pltpu.VMEM((16, 1024), bf16),
+            dma((6,)), dma((CHUNKS, 3)), dma((CHUNKS, 9)), dma((CHUNKS, 9)), dma((2,))],
         compiler_params=pltpu.CompilerParams(collective_id=2, has_side_effects=True),
         name="project",
-    )(x, wq, wk, wv, wz, wb, wa)
-
-
-def chain(t_of, b_of, sent, held, send_sem, recv_sem, after):
-    def hop(t, h):
-        return pltpu.make_async_remote_copy(
-            src_ref=sent.at[t, h], dst_ref=held.at[t, h], send_sem=send_sem.at[t, h],
-            recv_sem=recv_sem.at[t, h], device_id=after, device_id_type=MESH)
-
+    )(lens, dt, decay, x, wq, wk, wv, wz, wb, wa, tq, tk, tv)
+
+
+def hand_over(st_ref, s, g_out, g_in, t_out, t_in, b_in, r_out, r_in, h_send, h_recv):
+    x, y = s // SIDE, lax.rem(s, SIDE)
+    row = lambda j: x * SIDE + lax.rem(y + j, SIDE)
+    col = lambda j: lax.rem(x + j, SIDE) * SIDE + y
+
+    def to(k, src, dst, place):
+        return Later(lambda: pltpu.make_async_remote_copy(
+            src_ref=src, dst_ref=dst, send_sem=h_send.at[k], recv_sem=h_recv.at[k],
+            device_id={"seq": place}, device_id_type=MESH))
+
+    gather = [to(j - 1, g_out.at[lax.rem(y + j, SIDE)], g_in.at[j], row(j)) for j in (1, 2, 3)]
+    totals = [to(3, t_out, t_in, col(1)), to(4, t_out.at[:, :HD], b_in, col(2))]
+    back = [to(4 + j, r_out.at[lax.rem(y + j, SIDE)], r_in.at[j], row(j)) for j in (1, 2, 3)]
     for h in range(4):
-        sent[0, h] = b_of(h).astype(bf16)
-        hop(0, h).start()
-
-    def turn(t, carry):
-        for h in range(4):
-            hop(t - 1, h).wait_recv()
-            arrived = held[t - 1, h]
-            hi, lo = split2(t_of(h))
-            out = dotf(jnp.concatenate([hi, lo], axis=1),
-                       jnp.concatenate([arrived, arrived], axis=0)) + b_of(h)
-            sent[t, h] = out.astype(bf16)
-            hop(t, h).start()
-        return carry
-
-    lax.fori_loop(1, TURNS, turn, 0)
-    for h in range(4):
-        hop(TURNS - 1, h).wait_recv()
-
-    def drain(t, carry):
-        for h in range(4):
-            hop(t, h).wait_send()
-        return carry
-
-    return [held[TURNS - 1, h] for h in range(4)], lambda: lax.fori_loop(0, TURNS, drain, 0)
-
-
-def output_kernel(st_ref, o_hbm, l_hbm, raw_hbm, nw_ref, w_hbm, out_ref,
-                  o_v, l_v, z_v, w_v, sent, held, mine, theirs, given, pass_out, pass_in, to_up, to_down,
-                  from_down, from_up, load_sem, c_send, c_recv, p_send, p_recv, send_sem, recv_sem):
+        g_out[h] = st_ref[h].astype(bf16)
+    for j in (1, 0, 2):
+        gather[j].start()
+    g_in[0] = g_out[y]
+    for cp in gather:
+        cp.wait_recv()
+    prefix = [None, g_in[lax.rem(y + SIDE, SIDE)].astype(f32)]
+    for i in (1, 2, 3):
+        g = g_in[lax.rem(y + SIDE - i, SIDE)]
+        nxt = dotf(g[:, HD:], prefix[i].astype(bf16))
+        prefix.append(nxt + jnp.concatenate(
+            [g[:, :HD].astype(f32), jnp.zeros((HD, HD), f32)], axis=1))
+    t_out[...] = prefix[4].astype(bf16)
+    totals[1].start()
+    totals[0].start()
+    for cp in totals:
+        cp.wait_recv()
+    before = dotf(t_in[:, HD:], b_in[...]) + t_in[:, :HD].astype(f32)
+    before = before.astype(bf16)
+    r_out[0] = before
+    for i in (1, 2, 3):
+        r_out[i] = (prefix[i][:, :HD] + dotf(prefix[i][:, HD:].astype(bf16), before)).astype(bf16)
+    for j in (1, 0, 2):
+        back[j].start()
+    r_in[0] = r_out[y]
+    for cp in back:
+        cp.wait_recv()
+
+    def drain():
+        for cp in gather + totals + back:
+            cp.wait_send()
+
+    return [r_in[lax.rem(y + SIDE - h, SIDE)] for h in range(4)], drain
+
+
+def output_kernel(st_ref, o_hbm, l_hbm, z_hbm, nw_ref, w_hbm, out_ref,
+                  o_v, l_v, z_v, w_v, g_out, g_in, t_out, t_in, b_in, r_out, r_in, mine, theirs, given, pass_out, pass_in, to_up, to_down,
+                  from_down, from_up, load_sem, h_send, h_recv, p_send, p_recv, send_sem, recv_sem):
     h, z, c, up, down, far, mate = ring_places()
     s = lax.axis_index("seq")
     n = o_v.shape[0]
-    rc = n // CHUNKS
+    rc = n // OUT_CHUNKS
     half = rc // 2
     loads = [pltpu.make_async_copy(a, b, load_sem.at[i]) for i, (a, b) in enumerate((
-        (o_hbm, o_v), (l_hbm, l_v), (raw_hbm.at[:, 1024:1536], z_v), (w_hbm, w_v)))]
+        (o_hbm, o_v), (l_hbm, l_v), (z_hbm, z_v), (w_hbm, w_v)))]
     for cp in loads:
         cp.start()
-    after = {"seq": lax.rem(s + 1, SEQ)}
-    before = {"seq": lax.rem(s + SEQ - 1, SEQ)}
-    greet([{"head": up}, {"head": down}, {"head": mate}, after, before])
-    s_in, drained = chain(lambda i: st_ref[i, :, HD:], lambda i: st_ref[i, :, :HD],
-                          sent, held, c_send, c_recv, after)
+    x, y = s // SIDE, lax.rem(s, SIDE)
+    greet([{"head": up}, {"head": down}, {"head": mate}]
+          + [{"seq": x * SIDE + lax.rem(y + j, SIDE)} for j in (1, 2, 3)]
+          + [{"seq": lax.rem(x + j, SIDE) * SIDE + y} for j in (1, 2, 3)])
+    s_in, drained = hand_over(st_ref, s, g_out, g_in, t_out, t_in, b_in, r_out, r_in, h_send, h_recv)
     for cp in loads:
         cp.wait()
 
@@ -482,28 +528,28 @@
         out_ref[r * rc:(r + 1) * rc, :] = (
             both(r, 0) + from_down[r].astype(f32) + from_up[r].astype(f32)).astype(bf16)
 
-    for i in range(CHUNKS + 3):
-        if i < CHUNKS:
+    for i in range(OUT_CHUNKS + 5):
+        if i < OUT_CHUNKS:
             share(i)
-        if 1 <= i < CHUNKS + 1:
+        if 1 <= i < OUT_CHUNKS + 1:
             leave(i - 1)
-        if 2 <= i < CHUNKS + 2:
-            add_on(i - 2)
-        if i >= 3:
-            finish(i - 3)
+        if 3 <= i < OUT_CHUNKS + 3:
+            add_on(i - 3)
+        if i >= 5:
+            finish(i - 5)
     drained()
-    for r in range(CHUNKS):
+    for r in range(OUT_CHUNKS):
         for j in range(4):
             swap(r, j).wait_send()
         for cp in copies(r):
             cp.wait_send()
 
 
-def output(st, o, lift, raw, nw, w):
+def output(st, o, lift, z, nw, w):
     n = o.shape[0]
-    rc = n // CHUNKS
+    rc = n // OUT_CHUNKS
     vm, anyw = pl.BlockSpec(memory_space=pltpu.VMEM), pl.BlockSpec(memory_space=pl.ANY)
-    buf = pltpu.VMEM((CHUNKS, rc, 256), bf16)
+    buf = pltpu.VMEM((OUT_CHUNKS, rc, 256), bf16)
     dma = pltpu.SemaphoreType.DMA
     return pl.pallas_call(
         output_kernel,
@@ -511,23 +557,25 @@
         out_shape=jax.ShapeDtypeStruct((n, 256), bf16),
         scratch_shapes=[
             pltpu.VMEM((n, 512), f32), pltpu.VMEM((n, 512), bf16), pltpu.VMEM((n, 512), bf16),
-            pltpu.VMEM((512, 2048), bf16), pltpu.VMEM((TURNS, 4, HD, HD), bf16),
-            pltpu.VMEM((TURNS, 4, HD, HD), bf16), pltpu.VMEM((CHUNKS, 4, rc, 256), f32),
-            pltpu.VMEM((CHUNKS, 4, rc, 256), bf16), pltpu.VMEM((CHUNKS, 4, rc, 256), bf16),
+            pltpu.VMEM((512, 2048), bf16),
+            pltpu.VMEM((4, HD, 2 * HD), bf16), pltpu.VMEM((4, HD, 2 * HD), bf16),
+            pltpu.VMEM((HD, 2 * HD), bf16), pltpu.VMEM((HD, 2 * HD), bf16), pltpu.VMEM((HD, HD), bf16),
+            pltpu.VMEM((4, HD, HD), bf16), pltpu.VMEM((4, HD, HD), bf16), pltpu.VMEM((OUT_CHUNKS, 4, rc, 256), f32),
+            pltpu.VMEM((OUT_CHUNKS, 4, rc, 256), bf16), pltpu.VMEM((OUT_CHUNKS, 4, rc, 256), bf16),
             buf, buf, buf, buf, buf, buf,
-            dma((4,)), dma((TURNS, 4)), dma((TURNS, 4)), dma((CHUNKS, 4)), dma((CHUNKS, 4)),
-            dma((CHUNKS, 6)), dma((CHUNKS, 6))],
+            dma((4,)), dma((8,)), dma((8,)), dma((OUT_CHUNKS, 4)), dma((OUT_CHUNKS, 4)),
+            dma((OUT_CHUNKS, 6)), dma((OUT_CHUNKS, 6))],
         compiler_params=pltpu.CompilerParams(collective_id=3, has_side_effects=True),
         name="output",
-    )(st, o, lift, raw, nw, w)
+    )(st, o, lift, z, nw, w)
 
 
 def per_device(hidden_in, w_query, w_key, w_value, w_gate, w_beta, w_alpha, dt_bias, head_decay,
                conv_query, conv_key, conv_value, norm_weight, w_out, prompt_lengths):
-    raw, ba, halo = project(hidden_in, w_query, w_key, w_value, w_gate, w_beta, w_alpha)
-    o, lift, st = local_scan(prompt_lengths, dt_bias, head_decay, raw, halo, ba,
-                             conv_query, conv_key, conv_value)
-    return output(st, o, lift, raw, norm_weight[None, :], w_out)
+    o, lift, z, st = project(
+        prompt_lengths, dt_bias, head_decay, hidden_in, w_query, w_key, w_value, w_gate, w_beta.T,
+        w_alpha.T, conv_query, conv_key, conv_value)
+    return output(st, o, lift, z, norm_weight[None, :], w_out)
 
 
 def solution(mesh):

time: 124 us -> 98.9 us (0.80)
  Pallas kernels: 117 us -> 96.9 us
  local copies, waits for them, and re-layouts: 5.41 us -> 1.87 us
    pallas_call x1, Pallas kernels: 58.1 us -> 41.6 us  [output(): pl.pallas_call(output_kernel, in_specs=[vm, anyw, anyw, anyw, vm, anyw],...]
    pallas_call x2 -> x1, Pallas kernels: 59.3 us -> 55.3 us  [project(): pl.pallas_call(project_kernel, in_specs=[sm, sm, sm, vm] + [anyw] * 6 + [...]
    unnamed x3 -> x1, local copies, waits for them, and re-layouts: 5.41 us -> 1.87 us
where the time goes in v3:
time: 98.9 us; the launch traced here: 98.8 us
  Pallas kernels  96.9 us (98%)
  local copies, waits for them, and re-layouts  1.87 us (2%)
    pallas_call x1, Pallas kernels, project(): pl.pallas_call(project_kernel, in_specs=[sm, sm, sm, vm] + [anyw] * 6 + [...  55.3 us
    pallas_call x1, Pallas kernels, output(): pl.pallas_call(output_kernel, in_specs=[vm, anyw, anyw, anyw, vm, anyw],...  41.6 us

profile of v3, /device:TPU:0, one launch (start us, length us, event | category | flops | bytes accessed | tf_op | source)
XLA Modules:
  0.0 98.8 jit_solution(16035741961194061479)
XLA Ops:
  0.0 55.3 %project.1 = (f32[1024,512]{1,0:T(8,128)}, bf16[1024,512]{1,0:T(8,128)(2,1)}, bf16[1024,512]{1,0:T(8,128)(2,1)}, f32[4,128,256]{2,1,0:T(8,128)}) custom-call(s32[6]{0:T(128)} %lens.1, f32[4]{0:T(128)} %dt.1, f32[4]{0:T(128)} %decay.1, bf16[1024,256]{1,0:T(8,128)(2,1)} %x_ref.1, bf16[2048,256]{1,0:T(8,128)(2,1)} %wq.1, bf16[2048,256]{1,0:T(8,128)(2,1)} %wk.1, ...), custom_call_target="tpu_custom_call" | custom-call | tf_op jit(solution)/shard_map/project/pallas_call | solution.py:374
  55.3 41.6 %output.1 = bf16[1024,256]{1,0:T(8,128)(2,1)} custom-call(f32[4,128,256]{2,1,0:T(8,128)} %get-tuple-element.9.st_ref, f32[1024,512]{1,0:T(8,128)} %get-tuple-element.10.o_hbm, bf16[1024,512]{1,0:T(8,128)(2,1)} %get-tuple-element.11.l_hbm, bf16[1024,512]{1,0:T(8,128)(2,1)} %get-tuple-element.12.z_hbm, f32[1,128]{1,0:T(1,128)} %bitcast.5, bf16[512,2048]{1,0:T(8,128)(2,1)} %w_hbm.1), custom_call_target="tpu_custom_call" | custom-call | tf_op jit(solution)/shard_map/output/pallas_call | solution.py:554
  96.9 1.9 %copy.17 = bf16[1024,256]{1,0:T(8,128)(2,1)} copy(bf16[1024,256]{1,0:T(8,128)(2,1)} %output.1) | data formatting | bytes 1048576
